TPU v7x, 128 devices: a whole 4x4x4 slice. The times are simulated.
128 devices in a mesh: member: 8 (over z, core), band: 16 (over x, y).
Axes of the slice: x: 4, y: 4, z: 4, core: 2. Of those that a mesh axis runs over, the one named last changes fastest.
Arguments:
- latent: bfloat16 [8, 4096, 1024], P('member', 'band'), may hold values from -6 to 6
- observed: bfloat16 [4096, 128], P('band'), may hold values from -6 to 6
- area_weight: float32 [4096], P('band'), may hold values from 0.3 to 25, as said below
- band_counts: int32 [16], replicated, may hold values from 128 to 256, as said below
- gain_attn: float32 [1024], replicated, may hold values from 0.25 to 1.75
- w_query: bfloat16 [1024, 1024], replicated, may hold values from -0.1875 to 0.1875
- w_key: bfloat16 [1024, 1024], replicated, may hold values from -0.1875 to 0.1875
- w_value: bfloat16 [1024, 1024], replicated, may hold values from -0.1875 to 0.1875
- w_out: bfloat16 [1024, 1024], replicated, may hold values from -1.5 to 1.5
- gain_head: float32 [1024], replicated, may hold values from 0.25 to 1.75
- w_head: bfloat16 [1024, 128], replicated, may hold values from -0.1875 to 0.1875
Outputs:
- grad_latent: bfloat16 [8, 4096, 1024], P('member', 'band')
- grad_head: float32 [1024, 128], P('band')
- ensemble_loss: float32 [], replicated
Inputs may be any that keep to these rules, and one draw needn't show every extreme that they name: Band b holds band_counts[b] live grid points in its first slots; the remaining of its 256 slots are padding. In every draw some band holds exactly 256 and another exactly 128. `area_weight`: positive area weights.
All inputs are finite; a program needn't handle non-finite values.
Results may differ from a plain program's by a relative error of at most 0.019.
Values may be sent and summed in bfloat16 or wider, within the bound.
No kernel may reach another device: no remote copies, remote signals or barrier semaphores. Data moves between devices by JAX's collectives and lax.ppermute only.
A program may use at most 192 MiB of HBM per device.

v0:
```python
import math
import jax
import jax.numpy as jnp
from jax import lax
from jax.sharding import PartitionSpec as P

HEADS = 16
CH = 128
R = 512
HOPS = 4
NORM_EPS = 1e-06
SMOOTH_WIDTH = 0.25
FAIR_ALPHA = 0.95
heads_per_group = 4


def from_behind(value, axis, steps):
    count = lax.axis_size(axis)
    leading, last = (max(0, -steps), min(count, count - steps))
    return lax.ppermute(value, axis, [(source, source + steps) for source in range(leading, last)])


def inverse_rms(values):
    return lax.rsqrt(jnp.mean(values * values, axis=-1, keepdims=True) + NORM_EPS)


def norm_backward(values, gain_vec, inverse, upstream):
    scaled = upstream * gain_vec
    return inverse * scaled - values * inverse**3 * jnp.mean(
        values * scaled, axis=-1, keepdims=True
    )


def times_transposed(left_side, scaling_coefficient):
    return lax.dot_general(
        left_side,
        scaling_coefficient,
        (((left_side.ndim - 1,), (1,)), ((), ())),
        preferred_element_type=jnp.float32,
    )


def window_probs(query_group, key_group, allowed):
    head_size = query_group.shape[-1]
    scores = jnp.einsum(
        "mqgd,mkgd->mgqk", query_group, key_group, preferred_element_type=jnp.float32
    ) * (1.0 / math.sqrt(head_size))
    exponent = jnp.where(allowed[None, None], jnp.exp(scores), 0.0)
    return exponent / jnp.sum(exponent, axis=-1, keepdims=True)


def split_group(array_in, first_col, group_width, head_size):
    part_cols = lax.dynamic_slice_in_dim(array_in, first_col, group_width, 2)
    return part_cols.reshape(array_in.shape[0], array_in.shape[1], heads_per_group, head_size)


def attention_forward(queries, key_rows, value_rows, allowed):
    number_of_realizations, row_count, model_width = queries.shape
    head_size = model_width // HEADS
    group_width = heads_per_group * head_size

    def one_group(group_index, output):
        first_col = (group_index * group_width).astype(jnp.int32)
        query_group = split_group(queries, first_col, group_width, head_size)
        key_group = split_group(key_rows, first_col, group_width, head_size)
        value_group = split_group(value_rows, first_col, group_width, head_size)
        soft_b = window_probs(query_group, key_group, allowed).astype(jnp.bfloat16)
        mixed_group = jnp.einsum(
            "mgqk,mkgd->mqgd", soft_b, value_group, preferred_element_type=jnp.float32
        )
        mixed_group = mixed_group.reshape(number_of_realizations, row_count, group_width).astype(
            jnp.bfloat16
        )
        return lax.dynamic_update_slice_in_dim(output, mixed_group, first_col, 2)

    return lax.fori_loop(
        0, model_width // group_width, one_group, jnp.zeros(queries.shape, jnp.bfloat16)
    )


def attention_backward(queries, key_rows, value_rows, allowed, grad_mixed):
    number_of_realizations, row_count, model_width = queries.shape
    key_count = key_rows.shape[1]
    head_size = model_width // HEADS
    group_width = heads_per_group * head_size
    score_scale = 1.0 / math.sqrt(head_size)

    def one_group(group_index, carried):
        grad_query, grad_key, grad_value = carried
        first_col = (group_index * group_width).astype(jnp.int32)
        query_group = split_group(queries, first_col, group_width, head_size)
        key_group = split_group(key_rows, first_col, group_width, head_size)
        value_group = split_group(value_rows, first_col, group_width, head_size)
        upstream_group = split_group(grad_mixed, first_col, group_width, head_size)
        soft = window_probs(query_group, key_group, allowed)
        soft_b = soft.astype(jnp.bfloat16)
        d_soft = jnp.einsum(
            "mqgd,mkgd->mgqk", upstream_group, value_group, preferred_element_type=jnp.float32
        )
        inner_sum = jnp.sum(soft * d_soft, axis=-1, keepdims=True)
        d_score = (soft * (d_soft - inner_sum) * score_scale).astype(jnp.bfloat16)
        query_part = jnp.einsum(
            "mgqk,mkgd->mqgd", d_score, key_group, preferred_element_type=jnp.float32
        )
        key_part = jnp.einsum(
            "mgqk,mqgd->mkgd", d_score, query_group, preferred_element_type=jnp.float32
        )
        value_part = jnp.einsum(
            "mgqk,mqgd->mkgd", soft_b, upstream_group, preferred_element_type=jnp.float32
        )
        grad_query = lax.dynamic_update_slice_in_dim(
            grad_query,
            query_part.reshape(number_of_realizations, row_count, group_width).astype(jnp.bfloat16),
            first_col,
            2,
        )
        grad_key = lax.dynamic_update_slice_in_dim(
            grad_key,
            key_part.reshape(number_of_realizations, key_count, group_width).astype(jnp.bfloat16),
            first_col,
            2,
        )
        grad_value = lax.dynamic_update_slice_in_dim(
            grad_value,
            value_part.reshape(number_of_realizations, key_count, group_width).astype(jnp.bfloat16),
            first_col,
            2,
        )
        return (grad_query, grad_key, grad_value)

    initial = (
        jnp.zeros(queries.shape, jnp.bfloat16),
        jnp.zeros(key_rows.shape, jnp.bfloat16),
        jnp.zeros(value_rows.shape, jnp.bfloat16),
    )
    return lax.fori_loop(0, model_width // group_width, one_group, initial)


def probabilistic_accuracy(predicted_states, measured_part, scaling_coefficient):
    number_of_realizations = predicted_states.shape[0]
    fair_factor = 1.0 - (1.0 - FAIR_ALPHA) / number_of_realizations
    gap_from_measured = predicted_states - measured_part[None]
    smooth_observed = jnp.sqrt(gap_from_measured * gap_from_measured + SMOOTH_WIDTH * SMOOTH_WIDTH)
    between_realization_gap = predicted_states[:, None] - predicted_states[None, :]
    smooth_pair = jnp.sqrt(
        between_realization_gap * between_realization_gap + SMOOTH_WIDTH * SMOOTH_WIDTH
    )
    off_diagonal = (1.0 - jnp.eye(number_of_realizations, dtype=jnp.float32))[:, :, None, None]
    point_score = jnp.sum(smooth_observed, axis=0) / number_of_realizations - fair_factor / (
        2.0 * number_of_realizations * (number_of_realizations - 1)
    ) * jnp.sum(off_diagonal * smooth_pair, axis=(0, 1))
    total = jnp.sum(scaling_coefficient[:, None] * point_score)
    gradient = scaling_coefficient[None, :, None] * (
        gap_from_measured / smooth_observed / number_of_realizations
        - fair_factor
        / (number_of_realizations * (number_of_realizations - 1.0))
        * jnp.sum(between_realization_gap / smooth_pair, axis=1)
    )
    return (total, gradient)


def project_terms(key_part, value_part, w_key, w_value):
    return (times_transposed(key_part, w_key) + times_transposed(value_part, w_value)).astype(
        jnp.bfloat16
    )


def body(
    latent,
    observed,
    area_weight,
    band_counts,
    gain_attn,
    w_query,
    w_key,
    w_value,
    w_out,
    gain_head,
    w_head,
):
    band_index = lax.axis_index("band")
    band_total = lax.axis_size("band")
    member_total = lax.axis_size("member")
    members, slot_count, model_width = latent.shape
    hops = HOPS
    offsets_list = list(range(-hops, hops + 1))
    slot_iota = jnp.arange(slot_count, dtype=jnp.int32)
    offsets = jnp.cumsum(band_counts) - band_counts

    def band_rows(shift_by):
        other = band_index + shift_by
        inside = (other >= 0) & (other < band_total)
        clipped = jnp.clip(other, 0, band_total - 1)
        return (offsets[clipped] + slot_iota, inside & (slot_iota < band_counts[clipped]))

    own_pos, own_live = band_rows(0)
    key_pos = jnp.concatenate([band_rows(offset)[0] for offset in offsets_list])
    key_live = jnp.concatenate([band_rows(offset)[1] for offset in offsets_list])
    allowed = key_live[None, :] & (jnp.abs(own_pos[:, None] - key_pos[None, :]) <= R)
    latent_f = latent.astype(jnp.float32)
    inverse_one = inverse_rms(latent_f)
    normed = (latent_f * inverse_one * gain_attn).astype(jnp.bfloat16)
    queries = jnp.dot(normed, w_query, preferred_element_type=jnp.float32).astype(jnp.bfloat16)
    own_keys = jnp.dot(normed, w_key, preferred_element_type=jnp.float32).astype(jnp.bfloat16)
    own_values = jnp.dot(normed, w_value, preferred_element_type=jnp.float32).astype(jnp.bfloat16)
    key_parts = []
    value_parts = []
    for offset in offsets_list:
        if offset == 0:
            arrived = (own_keys, own_values)
        else:
            arrived = from_behind((own_keys, own_values), "band", -offset)
        key_parts.append(arrived[0])
        value_parts.append(arrived[1])
    key_rows = jnp.concatenate(key_parts, axis=1)
    value_rows = jnp.concatenate(value_parts, axis=1)
    mixed_out = attention_forward(queries, key_rows, value_rows, allowed)
    hidden = latent_f + jnp.dot(mixed_out, w_out, preferred_element_type=jnp.float32)
    inverse_two = inverse_rms(hidden)
    head_in = (hidden * inverse_two * gain_head).astype(jnp.bfloat16)
    predicted = jnp.dot(head_in, w_head, preferred_element_type=jnp.float32).astype(jnp.bfloat16)
    total_live = jnp.sum(band_counts).astype(jnp.float32) * CH
    point_weight = area_weight * own_live.astype(jnp.float32) / total_live
    grouped = lax.all_to_all(predicted, "member", split_axis=1, concat_axis=0, tiled=True)
    point_share = slot_count // member_total
    first_point = lax.axis_index("member") * point_share
    measured_part = lax.dynamic_slice_in_dim(observed, first_point, point_share, 0).astype(
        jnp.float32
    )
    weight_part = lax.dynamic_slice_in_dim(point_weight, first_point, point_share, 0)
    loss_part, gradient = probabilistic_accuracy(
        grouped.astype(jnp.float32), measured_part, weight_part
    )
    grad_pred = lax.all_to_all(
        gradient.astype(jnp.bfloat16), "member", split_axis=0, concat_axis=1, tiled=True
    )
    ensemble_loss = lax.psum(loss_part, ("member", "band"))
    head_share = lax.psum_scatter(
        lax.dot_general(
            head_in, grad_pred, (((0, 1), (0, 1)), ((), ())), preferred_element_type=jnp.float32
        ).astype(jnp.bfloat16),
        "band",
        scatter_dimension=0,
        tiled=True,
    )
    grad_head = lax.psum(head_share, "member").astype(jnp.float32)
    grad_hidden = norm_backward(hidden, gain_head, inverse_two, times_transposed(grad_pred, w_head))
    grad_mixed = times_transposed(grad_hidden.astype(jnp.bfloat16), w_out).astype(jnp.bfloat16)
    grad_queries, key_terms, value_terms = attention_backward(
        queries, key_rows, value_rows, allowed, grad_mixed
    )
    normed_total = jnp.zeros((members, slot_count, model_width), jnp.float32)
    for piece_index, offset in enumerate(offsets_list):
        key_piece = key_terms[:, piece_index * slot_count : (piece_index + 1) * slot_count]
        value_piece = value_terms[:, piece_index * slot_count : (piece_index + 1) * slot_count]
        if offset == 0:
            received = (key_piece, value_piece)
        else:
            received = from_behind((key_piece, value_piece), "band", offset)
        normed_piece = project_terms(received[0], received[1], w_key, w_value)
        normed_total = normed_total + normed_piece.astype(jnp.float32)
    grad_normed = times_transposed(grad_queries, w_query) + normed_total
    grad_latent = (
        grad_hidden + norm_backward(latent_f, gain_attn, inverse_one, grad_normed)
    ).astype(jnp.bfloat16)
    return (grad_latent, grad_head, ensemble_loss)


def solution(mesh):
    placed = (
        P("member", "band", None),
        P("band", None),
        P("band"),
        P(),
        P(),
        P(),
        P(),
        P(),
        P(),
        P(),
        P(),
    )
    return jax.shard_map(
        body,
        mesh=mesh,
        in_specs=placed,
        out_specs=(P("member", "band", None), P("band", None), P()),
        check_vma=False,
    )
```

profile of v0, /device:TPU:112, one launch (start us, length us, event | category | flops | bytes accessed | tf_op | source)
XLA Modules:
  0.0 862.6 jit_solution(12827514641480962040)
XLA Ops:
  16.2 4.6 collective-permute-start.10
  20.8 4.7 collective-permute-start.9
  58.5 10.5 %collective-permute-done.8 = bf16[1,256,1024]{2,1,0:T(8,128)(2,1)} collective-permute-done((bf16[1,256,1024]{2,1,0:T(8,128)(2,1)}, bf16[1,256,1024]{2,1,0:T(8,128)(2,1)}, u32[]{:S(2)}, u32[]{:S(2)}) %collective-permute-start.8) | collective-permute-done | bytes 524320 | tf_op jit(solution)/shard_map/ppermute | solution.py:20
  69.0 4.4 collective-permute-start
  88.0 11.4 %collective-permute-start.1 = (bf16[1,256,1024]{2,1,0:T(8,128)(2,1)S(1)}, bf16[1,256,1024]{2,1,0:T(8,128)(2,1)S(1)}, u32[]{:S(2)}, u32[]{:S(2)}) collective-permute-start(bf16[1,256,1024]{2,1,0:T(8,128)(2,1)S(1)} %copy-done.25), channel_id=1, source_target_pairs={{0,3},{1,4},{2,5},{3,6},{4,7},{5,8},{6,9},{7,10},{8,11},{9,12},{10... | collective-permute-start | bytes 1572872 | tf_op jit(solution)/shard_map/ppermute | solution.py:20
  100.3 6.0 collective-permute-start.2
  107.1 14.1 %collective-permute-done.13 = bf16[1,256,1024]{2,1,0:T(8,128)(2,1)S(1)} collective-permute-done((bf16[1,256,1024]{2,1,0:T(8,128)(2,1)}, bf16[1,256,1024]{2,1,0:T(8,128)(2,1)S(1)}, u32[]{:S(2)}, u32[]{:S(2)}) %collective-permute-start.13) | collective-permute-done | bytes 524320 | tf_op jit(solution)/shard_map/ppermute | solution.py:20
  126.9 6.6 collective-permute-start.4
  147.5 6.7 copy.42
  156.9 24.8 %collective-permute-done.5 = bf16[1,256,1024]{2,1,0:T(8,128)(2,1)S(1)} collective-permute-done((bf16[1,256,1024]{2,1,0:T(8,128)(2,1)S(1)}, bf16[1,256,1024]{2,1,0:T(8,128)(2,1)S(1)}, u32[]{:S(2)}, u32[]{:S(2)}) %collective-permute-start.5) | collective-permute-done | bytes 524320 | tf_op jit(solution)/shard_map/ppermute | solution.py:20
  186.3 6.7 copy.40
  193.1 39.2 %while.32 = (s32[]{:T(128)}, bf16[1,256,1024]{1,2,0:T(8,128)(2,1)S(1)}, bf16[1,2304,1024]{1,2,0:T(8,128)(2,1)}, bf16[1,256,1024]{1,2,0:T(8,128)(2,1)}, bf16[1,23...) while((s32[]{:T(128)}, ...), condition=%wide.region_4.5_spmd.clone, body=%wide.region_2.4_spmd.clone.sunk | while | flops 622918656 | bytes 28529072 | solution.py:76
  241.1 4.5 all-to-all-start
  254.9 5.4 all-to-all-start.1
  261.7 69.6 %psum.15 = f32[]{:T(128)} all-reduce(f32[]{:T(128)} %multiply_reduce_fusion.2), channel_id=1, replica_groups=mesh['member'=8,'band'=16] {'member','band'}, use_global_device_ids=true, to_apply=%region_19.20 | all-reduce | flops 1 | bytes 8 | tf_op jit(solution)/shard_map/psum | solution.py:237
  344.2 257.3 %while.33 = (s32[]{:T(128)}, bf16[1,256,1024]{1,2,0:T(8,128)(2,1)}, bf16[1,2304,1024]{1,2,0:T(8,128)(2,1)}, bf16[1,2304,1024]{1,2,0:T(8,128)(2,1)}, bf16[1,2304,...) while((s32[]{:T(128)}, bf16[1,256,1024]{1,2,0:T(8,128)(2,1)}, ...), condition=%wide.region_12.13_spmd.clone, body=%wide.region_9.12_spmd.clone.sunk | while | flops 1581979136 | bytes 88961552 | solution.py:136
  350.7 5.0 fusion.214
  355.7 5.6 fusion.216
  361.3 19.0 %fusion.217 = bf16[4,64,256]{2,1,0:T(8,128)(2,1)} fusion(bf16[2304,4,64]{0,2,1:T(8,128)(2,1)S(1)} %bitcast.244, f32[4,256,2304]{2,1,0:T(8,128)} %fusion.214, f32[4,256,2304]{2,1,0:T(8,128)} %get-tuple-element.631, f32[4,256]{1,0:T(4,128)} %get-tuple-element.632, pred[256,2304]{1,0:T(8,128)(4,1)} %copy-done.5), kind=kOutput, calls=%fused_computation.30.clone.1 | convolution fusion | flops 328011008 | bytes 20779008 | tf_op jit(solution)/shard_map/while/body/eval_jaxpr/mgqk,mkgd->mqgd/dot_general | solution.py:102
  380.3 19.6 %fusion.219 = bf16[4,64,2304]{2,1,0:T(8,128)(2,1)S(1)} fusion(bf16[256,4,64]{0,2,1:T(8,128)(2,1)S(1)} %bitcast.248, f32[4,256,2304]{2,1,0:T(8,128)} %fusion.214, f32[4,256,2304]{2,1,0:T(8,128)} %get-tuple-element.631, f32[4,256]{1,0:T(4,128)} %get-tuple-element.632, pred[256,2304]{1,0:T(8,128)(4,1)} %copy-done.5), kind=kOutput, calls=%fused_computation.27.clone.1 | convolution fusion | flops 328535296 | bytes 20779008 | tf_op jit(solution)/shard_map/while/body/eval_jaxpr/mgqk,mqgd->mkgd/dot_general | solution.py:105
  400.0 6.4 fusion.218
  415.0 5.0 fusion.214
  420.0 5.6 fusion.216
  425.6 19.0 %fusion.217 = bf16[4,64,256]{2,1,0:T(8,128)(2,1)} fusion(bf16[2304,4,64]{0,2,1:T(8,128)(2,1)S(1)} %bitcast.244, f32[4,256,2304]{2,1,0:T(8,128)} %fusion.214, f32[4,256,2304]{2,1,0:T(8,128)} %get-tuple-element.631, f32[4,256]{1,0:T(4,128)} %get-tuple-element.632, pred[256,2304]{1,0:T(8,128)(4,1)} %copy-done.5), kind=kOutput, calls=%fused_computation.30.clone.1 | convolution fusion | flops 328011008 | bytes 20779008 | tf_op jit(solution)/shard_map/while/body/eval_jaxpr/mgqk,mkgd->mqgd/dot_general | solution.py:102
  444.6 19.6 %fusion.219 = bf16[4,64,2304]{2,1,0:T(8,128)(2,1)S(1)} fusion(bf16[256,4,64]{0,2,1:T(8,128)(2,1)S(1)} %bitcast.248, f32[4,256,2304]{2,1,0:T(8,128)} %fusion.214, f32[4,256,2304]{2,1,0:T(8,128)} %get-tuple-element.631, f32[4,256]{1,0:T(4,128)} %get-tuple-element.632, pred[256,2304]{1,0:T(8,128)(4,1)} %copy-done.5), kind=kOutput, calls=%fused_computation.27.clone.1 | convolution fusion | flops 328535296 | bytes 20779008 | tf_op jit(solution)/shard_map/while/body/eval_jaxpr/mgqk,mqgd->mkgd/dot_general | solution.py:105
  464.3 6.4 fusion.218
  479.2 5.0 fusion.214
  484.2 5.6 fusion.216
  489.8 19.0 %fusion.217 = bf16[4,64,256]{2,1,0:T(8,128)(2,1)} fusion(bf16[2304,4,64]{0,2,1:T(8,128)(2,1)S(1)} %bitcast.244, f32[4,256,2304]{2,1,0:T(8,128)} %fusion.214, f32[4,256,2304]{2,1,0:T(8,128)} %get-tuple-element.631, f32[4,256]{1,0:T(4,128)} %get-tuple-element.632, pred[256,2304]{1,0:T(8,128)(4,1)} %copy-done.5), kind=kOutput, calls=%fused_computation.30.clone.1 | convolution fusion | flops 328011008 | bytes 20779008 | tf_op jit(solution)/shard_map/while/body/eval_jaxpr/mgqk,mkgd->mqgd/dot_general | solution.py:102
  508.8 19.6 %fusion.219 = bf16[4,64,2304]{2,1,0:T(8,128)(2,1)S(1)} fusion(bf16[256,4,64]{0,2,1:T(8,128)(2,1)S(1)} %bitcast.248, f32[4,256,2304]{2,1,0:T(8,128)} %fusion.214, f32[4,256,2304]{2,1,0:T(8,128)} %get-tuple-element.631, f32[4,256]{1,0:T(4,128)} %get-tuple-element.632, pred[256,2304]{1,0:T(8,128)(4,1)} %copy-done.5), kind=kOutput, calls=%fused_computation.27.clone.1 | convolution fusion | flops 328535296 | bytes 20779008 | tf_op jit(solution)/shard_map/while/body/eval_jaxpr/mgqk,mqgd->mkgd/dot_general | solution.py:105
  528.5 6.4 fusion.218
  543.4 5.0 fusion.214
  548.4 5.6 fusion.216
  554.0 19.0 %fusion.217 = bf16[4,64,256]{2,1,0:T(8,128)(2,1)} fusion(bf16[2304,4,64]{0,2,1:T(8,128)(2,1)S(1)} %bitcast.244, f32[4,256,2304]{2,1,0:T(8,128)} %fusion.214, f32[4,256,2304]{2,1,0:T(8,128)} %get-tuple-element.631, f32[4,256]{1,0:T(4,128)} %get-tuple-element.632, pred[256,2304]{1,0:T(8,128)(4,1)} %copy-done.5), kind=kOutput, calls=%fused_computation.30.clone.1 | convolution fusion | flops 328011008 | bytes 20779008 | tf_op jit(solution)/shard_map/while/body/eval_jaxpr/mgqk,mkgd->mqgd/dot_general | solution.py:102
  573.0 19.6 %fusion.219 = bf16[4,64,2304]{2,1,0:T(8,128)(2,1)S(1)} fusion(bf16[256,4,64]{0,2,1:T(8,128)(2,1)S(1)} %bitcast.248, f32[4,256,2304]{2,1,0:T(8,128)} %fusion.214, f32[4,256,2304]{2,1,0:T(8,128)} %get-tuple-element.631, f32[4,256]{1,0:T(4,128)} %get-tuple-element.632, pred[256,2304]{1,0:T(8,128)(4,1)} %copy-done.5), kind=kOutput, calls=%fused_computation.27.clone.1 | convolution fusion | flops 328535296 | bytes 20779008 | tf_op jit(solution)/shard_map/while/body/eval_jaxpr/mgqk,mqgd->mkgd/dot_general | solution.py:105
  592.7 6.4 fusion.218
  607.6 4.4 fusion.133
  613.3 5.4 collective-permute-start.29
  632.7 71.4 %reduce-scatter.2.cloned.1.call-done = bf16[64,128]{1,0:T(8,128)(2,1)} async-done(((bf16[1024,128]{1,0:T(8,128)(2,1)}), bf16[64,128]{1,0:T(8,128)(2,1)}) %reduce-scatter.2.cloned.1.call-update) | async-done | bytes 16400 | tf_op jit(solution)/shard_map/reduce_scatter | solution.py:238
  704.0 19.8 %psum.14 = bf16[64,128]{1,0:T(8,128)(2,1)S(1)} all-reduce(bf16[64,128]{1,0:T(8,128)(2,1)} %reduce-scatter.2.cloned.1.call-done), channel_id=1, replica_groups=mesh['member'=8,'band'=16] {'member'}, use_global_device_ids=true, to_apply=%region_15.16 | all-reduce | flops 8192 | bytes 32768 | tf_op jit(solution)/shard_map/psum | solution.py:246
  729.7 5.6 collective-permute-start.26
  741.1 18.3 %collective-permute-done.26 = bf16[1,256,1024]{1,2,0:T(8,128)(2,1)S(1)} collective-permute-done((bf16[1,256,1024]{1,2,0:T(8,128)(2,1)}, bf16[1,256,1024]{1,2,0:T(8,128)(2,1)S(1)}, u32[]{:S(2)}, u32[]{:S(2)}) %collective-permute-start.26) | collective-permute-done | bytes 524320 | tf_op jit(solution)/shard_map/ppermute | solution.py:20
  759.4 9.5 %collective-permute-start.24 = (bf16[1,256,1024]{1,2,0:T(8,128)(2,1)S(1)}, bf16[1,256,1024]{1,2,0:T(8,128)(2,1)S(1)}, u32[]{:S(2)}, u32[]{:S(2)}) collective-permute-start(bf16[1,256,1024]{1,2,0:T(8,128)(2,1)S(1)} %copy-done.24), channel_id=1, source_target_pairs={{0,1},{1,2},{2,3},{3,4},{4,5},{5,6},{6,7},{7,8},{8,9},{9,10},{10,1... | collective-permute-start | bytes 1572872 | tf_op jit(solution)/shard_map/ppermute | solution.py:20
  773.0 18.6 %collective-permute-done.24 = bf16[1,256,1024]{1,2,0:T(8,128)(2,1)S(1)} collective-permute-done((bf16[1,256,1024]{1,2,0:T(8,128)(2,1)S(1)}, bf16[1,256,1024]{1,2,0:T(8,128)(2,1)S(1)}, u32[]{:S(2)}, u32[]{:S(2)}) %collective-permute-start.24) | collective-permute-done | bytes 524320 | tf_op jit(solution)/shard_map/ppermute | solution.py:20
  797.7 9.7 %collective-permute-done.22 = bf16[1,256,1024]{1,2,0:T(8,128)(2,1)S(1)} collective-permute-done((bf16[1,256,1024]{1,2,0:T(8,128)(2,1)S(1)}, bf16[1,256,1024]{1,2,0:T(8,128)(2,1)S(1)}, u32[]{:S(2)}, u32[]{:S(2)}) %collective-permute-start.22) | collective-permute-done | bytes 524320 | tf_op jit(solution)/shard_map/ppermute | solution.py:20
  812.3 14.1 %collective-permute-done.20 = bf16[1,256,1024]{1,2,0:T(8,128)(2,1)S(1)} collective-permute-done((bf16[1,256,1024]{1,2,0:T(8,128)(2,1)S(1)}, bf16[1,256,1024]{1,2,0:T(8,128)(2,1)S(1)}, u32[]{:S(2)}, u32[]{:S(2)}) %collective-permute-start.20) | collective-permute-done | bytes 524320 | tf_op jit(solution)/shard_map/ppermute | solution.py:20
  828.6 8.1 collective-permute-start.30
  837.5 10.7 %collective-permute-done.18 = bf16[1,256,1024]{1,2,0:T(8,128)(2,1)S(1)} collective-permute-done((bf16[1,256,1024]{1,2,0:T(8,128)(2,1)S(1)}, bf16[1,256,1024]{1,2,0:T(8,128)(2,1)S(1)}, u32[]{:S(2)}, u32[]{:S(2)}) %collective-permute-start.18) | collective-permute-done | bytes 524320 | tf_op jit(solution)/shard_map/ppermute | solution.py:20
  (298 shorter events, 247.1 us)
Async XLA Ops:
  7.2 34.3 %copy-start.8 = (bf16[1,256,1024]{2,1,0:T(8,128)(2,1)S(1)}, bf16[1,256,1024]{2,1,0:T(8,128)(2,1)}, u32[]{:S(2)}) copy-start(bf16[1,256,1024]{2,1,0:T(8,128)(2,1)} %param.15) | copy-start | bytes 1572868
  7.2 34.2 %copy-start.32 = (f32[1024]{0:T(1024)S(1)}, f32[1024]{0:T(1024)}, u32[]{:S(2)}) copy-start(f32[1024]{0:T(1024)} %param.19) | copy-start | bytes 12292
  9.1 35.5 %copy-start.35 = (f32[256]{0:T(256)}, f32[256]{0:T(256)S(1)}, u32[]{:S(2)}) copy-start(f32[256]{0:T(256)S(1)} %get-tuple-element.465) | copy-start | bytes 3076
  9.1 40.5 %copy-start.37 = (f32[256]{0:T(256)S(1)}, f32[256]{0:T(256)}, u32[]{:S(2)}) copy-start(f32[256]{0:T(256)} %param.17) | copy-start | bytes 3076
  11.7 115.1 %collective-permute-start.15 = (bf16[1,256,1024]{2,1,0:T(8,128)(2,1)}, bf16[1,256,1024]{2,1,0:T(8,128)(2,1)S(1)}, u32[]{:S(2)}, u32[]{:S(2)}) collective-permute-start(bf16[1,256,1024]{2,1,0:T(8,128)(2,1)} %fusion.73), channel_id=1, source_target_pairs={{4,0},{5,1},{6,2},{7,3},{8,4},{9,5},{10,6},{11,7},{12,8},{13,9},{1... | collective-permute-start | bytes 1572872 | tf_op jit(solution)/shard_map/ppermute | solution.py:20
  13.0 69.9 %collective-permute-start.11 = (bf16[1,256,1024]{2,1,0:T(8,128)(2,1)}, bf16[1,256,1024]{2,1,0:T(8,128)(2,1)}, u32[]{:S(2)}, u32[]{:S(2)}) collective-permute-start(bf16[1,256,1024]{2,1,0:T(8,128)(2,1)} %fusion.73), channel_id=1, source_target_pairs={{0,1},{1,2},{2,3},{3,4},{4,5},{5,6},{6,7},{7,8},{8,9},{9,10},{10,1... | collective-permute-start | bytes 1572872 | tf_op jit(solution)/shard_map/ppermute | solution.py:20
  16.2 62.9 %collective-permute-start.10 = (bf16[1,256,1024]{2,1,0:T(8,128)(2,1)}, bf16[1,256,1024]{2,1,0:T(8,128)(2,1)}, u32[]{:S(2)}, u32[]{:S(2)}) collective-permute-start(bf16[1,256,1024]{2,1,0:T(8,128)(2,1)} %fusion.73), channel_id=1, source_target_pairs={{0,2},{1,3},{2,4},{3,5},{4,6},{5,7},{6,8},{7,9},{8,10},{9,11},{10,... | collective-permute-start | bytes 1572872 | tf_op jit(solution)/shard_map/ppermute | solution.py:20
  20.8 54.5 %collective-permute-start.9 = (bf16[1,256,1024]{2,1,0:T(8,128)(2,1)}, bf16[1,256,1024]{2,1,0:T(8,128)(2,1)}, u32[]{:S(2)}, u32[]{:S(2)}) collective-permute-start(bf16[1,256,1024]{2,1,0:T(8,128)(2,1)} %fusion.73), channel_id=1, source_target_pairs={{0,3},{1,4},{2,5},{3,6},{4,7},{5,8},{6,9},{7,10},{8,11},{9,12},{10... | collective-permute-start | bytes 1572872 | tf_op jit(solution)/shard_map/ppermute | solution.py:20
  25.5 43.5 %collective-permute-start.8 = (bf16[1,256,1024]{2,1,0:T(8,128)(2,1)}, bf16[1,256,1024]{2,1,0:T(8,128)(2,1)}, u32[]{:S(2)}, u32[]{:S(2)}) collective-permute-start(bf16[1,256,1024]{2,1,0:T(8,128)(2,1)} %fusion.73), channel_id=1, source_target_pairs={{0,4},{1,5},{2,6},{3,7},{4,8},{5,9},{6,10},{7,11},{8,12},{9,13},{1... | collective-permute-start | bytes 1572872 | tf_op jit(solution)/shard_map/ppermute | solution.py:20
  44.6 43.4 %copy-start.25 = (bf16[1,256,1024]{2,1,0:T(8,128)(2,1)S(1)}, bf16[1,256,1024]{2,1,0:T(8,128)(2,1)}, u32[]{:S(2)}) copy-start(bf16[1,256,1024]{2,1,0:T(8,128)(2,1)} %fusion.71) | copy-start | bytes 1572868
  69.0 18.9 %collective-permute-start = (bf16[1,256,1024]{2,1,0:T(8,128)(2,1)}, bf16[1,256,1024]{2,1,0:T(8,128)(2,1)S(1)}, u32[]{:S(2)}, u32[]{:S(2)}) collective-permute-start(bf16[1,256,1024]{2,1,0:T(8,128)(2,1)} %fusion.71), channel_id=1, source_target_pairs={{0,4},{1,5},{2,6},{3,7},{4,8},{5,9},{6,10},{7,11},{8,12},{9,13},{1... | collective-permute-start | bytes 1572872 | tf_op jit(solution)/shard_map/ppermute | solution.py:20
  75.3 24.9 %collective-permute-start.12 = (bf16[1,256,1024]{2,1,0:T(8,128)(2,1)}, bf16[1,256,1024]{2,1,0:T(8,128)(2,1)S(1)}, u32[]{:S(2)}, u32[]{:S(2)}) collective-permute-start(bf16[1,256,1024]{2,1,0:T(8,128)(2,1)} %fusion.73), channel_id=1, source_target_pairs={{1,0},{2,1},{3,2},{4,3},{5,4},{6,5},{7,6},{8,7},{9,8},{10,9},{11,1... | collective-permute-start | bytes 1572872 | tf_op jit(solution)/shard_map/ppermute | solution.py:20
  79.1 42.1 %collective-permute-start.13 = (bf16[1,256,1024]{2,1,0:T(8,128)(2,1)}, bf16[1,256,1024]{2,1,0:T(8,128)(2,1)S(1)}, u32[]{:S(2)}, u32[]{:S(2)}) collective-permute-start(bf16[1,256,1024]{2,1,0:T(8,128)(2,1)} %fusion.73), channel_id=1, source_target_pairs={{2,0},{3,1},{4,2},{5,3},{6,4},{7,5},{8,6},{9,7},{10,8},{11,9},{12,... | collective-permute-start | bytes 1572872 | tf_op jit(solution)/shard_map/ppermute | solution.py:20
  82.9 41.8 %collective-permute-start.14 = (bf16[1,256,1024]{2,1,0:T(8,128)(2,1)}, bf16[1,256,1024]{2,1,0:T(8,128)(2,1)S(1)}, u32[]{:S(2)}, u32[]{:S(2)}) collective-permute-start(bf16[1,256,1024]{2,1,0:T(8,128)(2,1)} %fusion.73), channel_id=1, source_target_pairs={{3,0},{4,1},{5,2},{6,3},{7,4},{8,5},{9,6},{10,7},{11,8},{12,9},{13... | collective-permute-start | bytes 1572872 | tf_op jit(solution)/shard_map/ppermute | solution.py:20
  88.0 46.4 %collective-permute-start.1 = (bf16[1,256,1024]{2,1,0:T(8,128)(2,1)S(1)}, bf16[1,256,1024]{2,1,0:T(8,128)(2,1)S(1)}, u32[]{:S(2)}, u32[]{:S(2)}) collective-permute-start(bf16[1,256,1024]{2,1,0:T(8,128)(2,1)S(1)} %copy-done.25), channel_id=1, source_target_pairs={{0,3},{1,4},{2,5},{3,6},{4,7},{5,8},{6,9},{7,10},{8,11},{9,12},{10... | collective-permute-start | bytes 1572872 | tf_op jit(solution)/shard_map/ppermute | solution.py:20
  100.3 39.9 %collective-permute-start.2 = (bf16[1,256,1024]{2,1,0:T(8,128)(2,1)S(1)}, bf16[1,256,1024]{2,1,0:T(8,128)(2,1)S(1)}, u32[]{:S(2)}, u32[]{:S(2)}) collective-permute-start(bf16[1,256,1024]{2,1,0:T(8,128)(2,1)S(1)} %copy-done.25), channel_id=1, source_target_pairs={{0,2},{1,3},{2,4},{3,5},{4,6},{5,7},{6,8},{7,9},{8,10},{9,11},{10,... | collective-permute-start | bytes 1572872 | tf_op jit(solution)/shard_map/ppermute | solution.py:20
  121.2 25.4 %collective-permute-start.3 = (bf16[1,256,1024]{2,1,0:T(8,128)(2,1)S(1)}, bf16[1,256,1024]{2,1,0:T(8,128)(2,1)S(1)}, u32[]{:S(2)}, u32[]{:S(2)}) collective-permute-start(bf16[1,256,1024]{2,1,0:T(8,128)(2,1)S(1)} %copy-done.25), channel_id=1, source_target_pairs={{0,1},{1,2},{2,3},{3,4},{4,5},{5,6},{6,7},{7,8},{8,9},{9,10},{10,1... | collective-permute-start | bytes 1572872 | tf_op jit(solution)/shard_map/ppermute | solution.py:20
  124.7 59.7 %collective-permute-start.7 = (bf16[1,256,1024]{2,1,0:T(8,128)(2,1)S(1)}, bf16[1,256,1024]{2,1,0:T(8,128)(2,1)}, u32[]{:S(2)}, u32[]{:S(2)}) collective-permute-start(bf16[1,256,1024]{2,1,0:T(8,128)(2,1)S(1)} %copy-done.25), channel_id=1, source_target_pairs={{4,0},{5,1},{6,2},{7,3},{8,4},{9,5},{10,6},{11,7},{12,8},{13,9},{1... | collective-permute-start | bytes 1572872 | tf_op jit(solution)/shard_map/ppermute | solution.py:20
  126.9 28.2 %collective-permute-start.4 = (bf16[1,256,1024]{2,1,0:T(8,128)(2,1)S(1)}, bf16[1,256,1024]{2,1,0:T(8,128)(2,1)}, u32[]{:S(2)}, u32[]{:S(2)}) collective-permute-start(bf16[1,256,1024]{2,1,0:T(8,128)(2,1)S(1)} %copy-done.25), channel_id=1, source_target_pairs={{1,0},{2,1},{3,2},{4,3},{5,4},{6,5},{7,6},{8,7},{9,8},{10,9},{11,1... | collective-permute-start | bytes 1572872 | tf_op jit(solution)/shard_map/ppermute | solution.py:20
  134.3 47.4 %collective-permute-start.5 = (bf16[1,256,1024]{2,1,0:T(8,128)(2,1)S(1)}, bf16[1,256,1024]{2,1,0:T(8,128)(2,1)S(1)}, u32[]{:S(2)}, u32[]{:S(2)}) collective-permute-start(bf16[1,256,1024]{2,1,0:T(8,128)(2,1)S(1)} %copy-done.25), channel_id=1, source_target_pairs={{2,0},{3,1},{4,2},{5,3},{6,4},{7,5},{8,6},{9,7},{10,8},{11,9},{12,... | collective-permute-start | bytes 1572872 | tf_op jit(solution)/shard_map/ppermute | solution.py:20
  140.1 42.4 %collective-permute-start.6 = (bf16[1,256,1024]{2,1,0:T(8,128)(2,1)S(1)}, bf16[1,256,1024]{2,1,0:T(8,128)(2,1)}, u32[]{:S(2)}, u32[]{:S(2)}) collective-permute-start(bf16[1,256,1024]{2,1,0:T(8,128)(2,1)S(1)} %copy-done.25), channel_id=1, source_target_pairs={{3,0},{4,1},{5,2},{6,3},{7,4},{8,5},{9,6},{10,7},{11,8},{12,9},{13... | collective-permute-start | bytes 1572872 | tf_op jit(solution)/shard_map/ppermute | solution.py:20
  193.1 43.9 %copy-start.15 = (bf16[1024,128]{1,0:T(8,128)(2,1)S(1)}, bf16[1024,128]{1,0:T(8,128)(2,1)}, u32[]{:S(2)}) copy-start(bf16[1024,128]{1,0:T(8,128)(2,1)} %param.25) | copy-start | bytes 786436
  193.1 43.9 %copy-start.26 = (f32[1024]{0:T(1024)S(1)}, f32[1024]{0:T(1024)}, u32[]{:S(2)}) copy-start(f32[1024]{0:T(1024)} %param.24) | copy-start | bytes 12292
  235.8 102.6 %copy-start.3 = (f32[1,256,1024]{2,1,0:T(8,128)}, f32[1,256,1024]{2,1,0:T(8,128)S(1)}, u32[]{:S(2)}) copy-start(f32[1,256,1024]{2,1,0:T(8,128)S(1)} %get-tuple-element.489) | copy-start | bytes 3145732
  241.1 8.1 all-to-all-start
  254.9 76.4 %all-to-all-start.1 = ((bf16[8,32,128]{2,1,0:T(8,128)(2,1)}), bf16[8,32,128]{2,1,0:T(8,128)(2,1)S(1)}, u32[]{:S(2)}, u32[]{:S(2)}) async-start(bf16[8,32,128]{2,1,0:T(8,128)(2,1)} %get-tuple-element.463), calls=%async_computation.1 | async-start | bytes 131072 | tf_op jit(solution)/shard_map/all_to_all | solution.py:234
  260.3 443.7 %reduce-scatter.2.cloned.1.call-start = ((), (), s32[]{:S(2)}) async-start(), calls=%async_computation.3 | async-start | bytes 278528 | tf_op jit(solution)/shard_map/reduce_scatter | solution.py:238
  612.0 237.0 %collective-permute-start.17 = (bf16[1,256,1024]{1,2,0:T(8,128)(2,1)}, bf16[1,256,1024]{1,2,0:T(8,128)(2,1)}, u32[]{:S(2)}, u32[]{:S(2)}) collective-permute-start(bf16[1,256,1024]{1,2,0:T(8,128)(2,1)} %get-tuple-element.454), channel_id=1, source_target_pairs={{4,0},{5,1},{6,2},{7,3},{8,4},{9,5},{10,6},{11,7},{12,8},{13,9},{1... | collective-permute-start | bytes 1572872 | tf_op jit(solution)/shard_map/ppermute | solution.py:20
  613.3 111.2 %collective-permute-start.29 = (bf16[1,256,1024]{1,2,0:T(8,128)(2,1)}, bf16[1,256,1024]{1,2,0:T(8,128)(2,1)}, u32[]{:S(2)}, u32[]{:S(2)}) collective-permute-start(bf16[1,256,1024]{1,2,0:T(8,128)(2,1)} %get-tuple-element.455), channel_id=1, source_target_pairs={{0,3},{1,4},{2,5},{3,6},{4,7},{5,8},{6,9},{7,10},{8,11},{9,12},{10... | collective-permute-start | bytes 1572872 | tf_op jit(solution)/shard_map/ppermute | solution.py:20
  618.8 118.4 %collective-permute-start.27 = (bf16[1,256,1024]{1,2,0:T(8,128)(2,1)}, bf16[1,256,1024]{1,2,0:T(8,128)(2,1)}, u32[]{:S(2)}, u32[]{:S(2)}) collective-permute-start(bf16[1,256,1024]{1,2,0:T(8,128)(2,1)} %get-tuple-element.456), channel_id=1, source_target_pairs={{0,2},{1,3},{2,4},{3,5},{4,6},{5,7},{6,8},{7,9},{8,10},{9,11},{10,... | collective-permute-start | bytes 1572872 | tf_op jit(solution)/shard_map/ppermute | solution.py:20
  621.6 148.1 %collective-permute-start.25 = (bf16[1,256,1024]{1,2,0:T(8,128)(2,1)}, bf16[1,256,1024]{1,2,0:T(8,128)(2,1)}, u32[]{:S(2)}, u32[]{:S(2)}) collective-permute-start(bf16[1,256,1024]{1,2,0:T(8,128)(2,1)} %get-tuple-element.457), channel_id=1, source_target_pairs={{0,1},{1,2},{2,3},{3,4},{4,5},{5,6},{6,7},{7,8},{8,9},{9,10},{10,1... | collective-permute-start | bytes 1572872 | tf_op jit(solution)/shard_map/ppermute | solution.py:20
  625.1 104.6 %collective-permute-start.28 = (bf16[1,256,1024]{1,2,0:T(8,128)(2,1)}, bf16[1,256,1024]{1,2,0:T(8,128)(2,1)}, u32[]{:S(2)}, u32[]{:S(2)}) collective-permute-start(bf16[1,256,1024]{1,2,0:T(8,128)(2,1)} %get-tuple-element.447), channel_id=1, source_target_pairs={{0,3},{1,4},{2,5},{3,6},{4,7},{5,8},{6,9},{7,10},{8,11},{9,12},{10... | collective-permute-start | bytes 1572872 | tf_op jit(solution)/shard_map/ppermute | solution.py:20
  724.5 70.1 %collective-permute-start.23 = (bf16[1,256,1024]{1,2,0:T(8,128)(2,1)}, bf16[1,256,1024]{1,2,0:T(8,128)(2,1)S(1)}, u32[]{:S(2)}, u32[]{:S(2)}) collective-permute-start(bf16[1,256,1024]{1,2,0:T(8,128)(2,1)} %get-tuple-element.458), channel_id=1, source_target_pairs={{1,0},{2,1},{3,2},{4,3},{5,4},{6,5},{7,6},{8,7},{9,8},{10,9},{11,1... | collective-permute-start | bytes 1572872 | tf_op jit(solution)/shard_map/ppermute | solution.py:20
  729.7 29.7 %copy-start.24 = (bf16[1,256,1024]{1,2,0:T(8,128)(2,1)S(1)}, bf16[1,256,1024]{1,2,0:T(8,128)(2,1)}, u32[]{:S(2)}) copy-start(bf16[1,256,1024]{1,2,0:T(8,128)(2,1)} %get-tuple-element.449) | copy-start | bytes 1572868
  729.7 29.7 %collective-permute-start.26 = (bf16[1,256,1024]{1,2,0:T(8,128)(2,1)}, bf16[1,256,1024]{1,2,0:T(8,128)(2,1)S(1)}, u32[]{:S(2)}, u32[]{:S(2)}) collective-permute-start(bf16[1,256,1024]{1,2,0:T(8,128)(2,1)} %get-tuple-element.448), channel_id=1, source_target_pairs={{0,2},{1,3},{2,4},{3,5},{4,6},{5,7},{6,8},{7,9},{8,10},{9,11},{10,... | collective-permute-start | bytes 1572872 | tf_op jit(solution)/shard_map/ppermute | solution.py:20
  737.2 32.6 %copy-start.21 = (bf16[1,256,1024]{1,2,0:T(8,128)(2,1)S(1)}, bf16[1,256,1024]{1,2,0:T(8,128)(2,1)}, u32[]{:S(2)}) copy-start(bf16[1,256,1024]{1,2,0:T(8,128)(2,1)} %get-tuple-element.460) | copy-start | bytes 1572868
  737.2 72.9 %collective-permute-start.21 = (bf16[1,256,1024]{1,2,0:T(8,128)(2,1)S(1)}, bf16[1,256,1024]{1,2,0:T(8,128)(2,1)S(1)}, u32[]{:S(2)}, u32[]{:S(2)}) collective-permute-start(bf16[1,256,1024]{1,2,0:T(8,128)(2,1)S(1)} %copy-done.23), channel_id=1, source_target_pairs={{2,0},{3,1},{4,2},{5,3},{6,4},{7,5},{8,6},{9,7},{10,8},{11,9},{12,... | collective-permute-start | bytes 1572872 | tf_op jit(solution)/shard_map/ppermute | solution.py:20
  741.1 50.6 %copy-start.22 = (bf16[1,256,1024]{1,2,0:T(8,128)(2,1)S(1)}, bf16[1,256,1024]{1,2,0:T(8,128)(2,1)}, u32[]{:S(2)}) copy-start(bf16[1,256,1024]{1,2,0:T(8,128)(2,1)} %get-tuple-element.450) | copy-start | bytes 1572868
  759.4 32.2 %collective-permute-start.24 = (bf16[1,256,1024]{1,2,0:T(8,128)(2,1)S(1)}, bf16[1,256,1024]{1,2,0:T(8,128)(2,1)S(1)}, u32[]{:S(2)}, u32[]{:S(2)}) collective-permute-start(bf16[1,256,1024]{1,2,0:T(8,128)(2,1)S(1)} %copy-done.24), channel_id=1, source_target_pairs={{0,1},{1,2},{2,3},{3,4},{4,5},{5,6},{6,7},{7,8},{8,9},{9,10},{10,1... | collective-permute-start | bytes 1572872 | tf_op jit(solution)/shard_map/ppermute | solution.py:20
  769.7 58.8 %collective-permute-start.19 = (bf16[1,256,1024]{1,2,0:T(8,128)(2,1)S(1)}, bf16[1,256,1024]{1,2,0:T(8,128)(2,1)S(1)}, u32[]{:S(2)}, u32[]{:S(2)}) collective-permute-start(bf16[1,256,1024]{1,2,0:T(8,128)(2,1)S(1)} %copy-done.21), channel_id=1, source_target_pairs={{3,0},{4,1},{5,2},{6,3},{7,4},{8,5},{9,6},{10,7},{11,8},{12,9},{13... | collective-permute-start | bytes 1572872 | tf_op jit(solution)/shard_map/ppermute | solution.py:20
  773.0 34.4 %copy-start.20 = (bf16[1,256,1024]{1,2,0:T(8,128)(2,1)S(1)}, bf16[1,256,1024]{1,2,0:T(8,128)(2,1)}, u32[]{:S(2)}) copy-start(bf16[1,256,1024]{1,2,0:T(8,128)(2,1)} %get-tuple-element.451) | copy-start | bytes 1572868
  791.6 15.8 %collective-permute-start.22 = (bf16[1,256,1024]{1,2,0:T(8,128)(2,1)S(1)}, bf16[1,256,1024]{1,2,0:T(8,128)(2,1)S(1)}, u32[]{:S(2)}, u32[]{:S(2)}) collective-permute-start(bf16[1,256,1024]{1,2,0:T(8,128)(2,1)S(1)} %copy-done.22), channel_id=1, source_target_pairs={{1,0},{2,1},{3,2},{4,3},{5,4},{6,5},{7,6},{8,7},{9,8},{10,9},{11,1... | collective-permute-start | bytes 1572872 | tf_op jit(solution)/shard_map/ppermute | solution.py:20
  794.7 56.2 %collective-permute-start.31 = (bf16[1,256,1024]{1,2,0:T(8,128)(2,1)S(1)}, bf16[1,256,1024]{1,2,0:T(8,128)(2,1)S(1)}, u32[]{:S(2)}, u32[]{:S(2)}) collective-permute-start(bf16[1,256,1024]{1,2,0:T(8,128)(2,1)S(1)} %copy-done.19), channel_id=1, source_target_pairs={{0,4},{1,5},{2,6},{3,7},{4,8},{5,9},{6,10},{7,11},{8,12},{9,13},{1... | collective-permute-start | bytes 1572872 | tf_op jit(solution)/shard_map/ppermute | solution.py:20
  797.7 28.8 %copy-start.18 = (bf16[1,256,1024]{1,2,0:T(8,128)(2,1)S(1)}, bf16[1,256,1024]{1,2,0:T(8,128)(2,1)}, u32[]{:S(2)}) copy-start(bf16[1,256,1024]{1,2,0:T(8,128)(2,1)} %get-tuple-element.452) | copy-start | bytes 1572868
  807.4 19.1 %collective-permute-start.20 = (bf16[1,256,1024]{1,2,0:T(8,128)(2,1)S(1)}, bf16[1,256,1024]{1,2,0:T(8,128)(2,1)S(1)}, u32[]{:S(2)}, u32[]{:S(2)}) collective-permute-start(bf16[1,256,1024]{1,2,0:T(8,128)(2,1)S(1)} %copy-done.20), channel_id=1, source_target_pairs={{2,0},{3,1},{4,2},{5,3},{6,4},{7,5},{8,6},{9,7},{10,8},{11,9},{12,... | collective-permute-start | bytes 1572872 | tf_op jit(solution)/shard_map/ppermute | solution.py:20
  810.1 42.4 %collective-permute-start.16 = (bf16[1,256,1024]{1,2,0:T(8,128)(2,1)S(1)}, bf16[1,256,1024]{1,2,0:T(8,128)(2,1)S(1)}, u32[]{:S(2)}, u32[]{:S(2)}) collective-permute-start(bf16[1,256,1024]{1,2,0:T(8,128)(2,1)S(1)} %copy-done.16), channel_id=1, source_target_pairs={{4,0},{5,1},{6,2},{7,3},{8,4},{9,5},{10,6},{11,7},{12,8},{13,9},{1... | collective-permute-start | bytes 1572872 | tf_op jit(solution)/shard_map/ppermute | solution.py:20
  826.5 21.7 %collective-permute-start.18 = (bf16[1,256,1024]{1,2,0:T(8,128)(2,1)S(1)}, bf16[1,256,1024]{1,2,0:T(8,128)(2,1)S(1)}, u32[]{:S(2)}, u32[]{:S(2)}) collective-permute-start(bf16[1,256,1024]{1,2,0:T(8,128)(2,1)S(1)} %copy-done.18), channel_id=1, source_target_pairs={{3,0},{4,1},{5,2},{6,3},{7,4},{8,5},{9,6},{10,7},{11,8},{12,9},{13... | collective-permute-start | bytes 1572872 | tf_op jit(solution)/shard_map/ppermute | solution.py:20
  828.6 23.1 %collective-permute-start.30 = (bf16[1,256,1024]{1,2,0:T(8,128)(2,1)S(1)}, bf16[1,256,1024]{1,2,0:T(8,128)(2,1)S(1)}, u32[]{:S(2)}, u32[]{:S(2)}) collective-permute-start(bf16[1,256,1024]{1,2,0:T(8,128)(2,1)S(1)} %copy-done.17), channel_id=1, source_target_pairs={{0,4},{1,5},{2,6},{3,7},{4,8},{5,9},{6,10},{7,11},{8,12},{9,13},{1... | collective-permute-start | bytes 1572872 | tf_op jit(solution)/shard_map/ppermute | solution.py:20
  (31 other events, 243.3 us)
Sparse Core Ops, SparseCore 0:
  607.7 96.3 reduce-scatter.1
where the time goes:
time: 871 us; the launch traced here: 863 us
  matrix products  288 us (33%)
  waiting for transfers between devices  203 us (23%)
  starting transfers between devices  123 us (14%)
  local copies, waits for them, and re-layouts  103 us (12%)
  blocking collectives  89.4 us (10%)
  other arithmetic  39.8 us (5%)
  between operations  16.2 us (2%)
    ppermute x32, waiting for transfers between devices, from_behind(): lax.ppermute(value, axis, [(source, source + steps) for source in range(l...  129 us
    ppermute x32, starting transfers between devices, from_behind(): lax.ppermute(value, axis, [(source, source + steps) for source in range(l...  113 us
    dot_general x4, matrix products, one_group(): jnp.einsum('mgqk,mqgd->mkgd', d_score, query_group, preferred_element_typ...  78.6 us
    dot_general x4, matrix products, one_group(): jnp.einsum('mgqk,mkgd->mqgd', d_score, key_group, preferred_element_type=...  76.1 us
    reduce_scatter x1, waiting for transfers between devices, body(): lax.psum_scatter(lax.dot_general(head_in, grad_pred, (((0, 1), (0, 1)), (...  71.4 us
    psum x1, blocking collectives, body(): ensemble_loss = lax.psum(loss_part, ('member', 'band'))  69.6 us
    unnamed x102, local copies, waits for them, and re-layouts  43.2 us
    dot_general x8, matrix products, window_probs(): jnp.einsum('mqgd,mkgd->mgqk', query_group, key_group, preferred_element_t...  33.4 us
  transfers between devices with their start and end apart: 35, of which 13 were waited for; matrix products, arithmetic and copies ran while one was open for 10% of the time, Pallas kernels for 0%

commit v1 on v0

--- a/solution.py
+++ b/solution.py
@@ -243,7 +243,7 @@
         scatter_dimension=0,
         tiled=True,
     )
-    grad_head = lax.psum(head_share, "member").astype(jnp.float32)
+    grad_head = jnp.sum(lax.all_gather(head_share, "member"), axis=0).astype(jnp.float32)
     grad_hidden = norm_backward(hidden, gain_head, inverse_two, times_transposed(grad_pred, w_head))
     grad_mixed = times_transposed(grad_hidden.astype(jnp.bfloat16), w_out).astype(jnp.bfloat16)
     grad_queries, key_terms, value_terms = attention_backward(

time: 871 us -> 793 us (0.910)
  waiting for transfers between devices: 203 us -> 129 us
    reduce_scatter x1, waiting for transfers between devices: 71.4 us -> 0.02 us  [body(): lax.psum_scatter(lax.dot_general(head_in, grad_pred, (((0, 1), (0, 1)), (...]
    psum x1 -> x0, blocking collectives: 19.8 us -> none  [body(): grad_head = lax.psum(head_share, 'member').astype(jnp.float32)]
    all_gather x0 -> x1, blocking collectives: none -> 13 us  [body(): lax.all_gather(head_share, 'member')]
    unnamed x102 -> x104, local copies, waits for them, and re-layouts: 43.2 us -> 42.2 us
  transfers between devices with their start and end apart: 35 -> 35, of which waited for: 13 -> 12; matrix products, arithmetic and copies ran while one was open for 10% -> 45% of each run, Pallas kernels for 0% -> 0%
where the time goes in v1:
time: 793 us; the launch traced here: 782 us
  matrix products  289 us (36%)
  waiting for transfers between devices  129 us (16%)
  starting transfers between devices  125 us (16%)
  local copies, waits for them, and re-layouts  99.7 us (13%)
  blocking collectives  82.5 us (10%)
  other arithmetic  39.9 us (5%)
  between operations  16.2 us (2%)
    ppermute x32, waiting for transfers between devices, from_behind(): lax.ppermute(value, axis, [(source, source + steps) for source in range(l...  126 us
    ppermute x32, starting transfers between devices, from_behind(): lax.ppermute(value, axis, [(source, source + steps) for source in range(l...  115 us
    dot_general x4, matrix products, one_group(): jnp.einsum('mgqk,mqgd->mkgd', d_score, query_group, preferred_element_typ...  78.4 us
    dot_general x4, matrix products, one_group(): jnp.einsum('mgqk,mkgd->mqgd', d_score, key_group, preferred_element_type=...  76 us
    psum x1, blocking collectives, body(): ensemble_loss = lax.psum(loss_part, ('member', 'band'))  69.6 us
    unnamed x104, local copies, waits for them, and re-layouts  42.2 us
    dot_general x8, matrix products, window_probs(): jnp.einsum('mqgd,mkgd->mgqk', query_group, key_group, preferred_element_t...  33.1 us
    dynamic_slice x28, local copies, waits for them, and re-layouts, split_group(): part_cols = lax.dynamic_slice_in_dim(array_in, first_col, group_width, 2)  30.3 us
  transfers between devices with their start and end apart: 35, of which 12 were waited for; matrix products, arithmetic and copies ran while one was open for 45% of the time, Pallas kernels for 0%

profile of v1, /device:TPU:112, one launch (start us, length us, event | category | flops | bytes accessed | tf_op | source)
XLA Modules:
  0.0 781.5 jit_solution(10943750812590681687)
XLA Ops:
  16.3 4.6 collective-permute-start.10
  20.9 4.7 collective-permute-start.9
  58.5 10.6 %collective-permute-done.8 = bf16[1,256,1024]{2,1,0:T(8,128)(2,1)} collective-permute-done((bf16[1,256,1024]{2,1,0:T(8,128)(2,1)}, bf16[1,256,1024]{2,1,0:T(8,128)(2,1)}, u32[]{:S(2)}, u32[]{:S(2)}) %collective-permute-start.8) | collective-permute-done | bytes 524320 | tf_op jit(solution)/shard_map/ppermute | solution.py:20
  69.1 4.4 collective-permute-start
  88.0 11.4 %collective-permute-start.1 = (bf16[1,256,1024]{2,1,0:T(8,128)(2,1)S(1)}, bf16[1,256,1024]{2,1,0:T(8,128)(2,1)S(1)}, u32[]{:S(2)}, u32[]{:S(2)}) collective-permute-start(bf16[1,256,1024]{2,1,0:T(8,128)(2,1)S(1)} %copy-done.24), channel_id=1, source_target_pairs={{0,3},{1,4},{2,5},{3,6},{4,7},{5,8},{6,9},{7,10},{8,11},{9,12},{10... | collective-permute-start | bytes 1572872 | tf_op jit(solution)/shard_map/ppermute | solution.py:20
  100.3 6.0 collective-permute-start.2
  107.2 14.2 %collective-permute-done.13 = bf16[1,256,1024]{2,1,0:T(8,128)(2,1)S(1)} collective-permute-done((bf16[1,256,1024]{2,1,0:T(8,128)(2,1)}, bf16[1,256,1024]{2,1,0:T(8,128)(2,1)S(1)}, u32[]{:S(2)}, u32[]{:S(2)}) %collective-permute-start.13) | collective-permute-done | bytes 524320 | tf_op jit(solution)/shard_map/ppermute | solution.py:20
  126.9 6.7 collective-permute-start.4
  147.5 6.7 copy.42
  156.9 24.9 %collective-permute-done.5 = bf16[1,256,1024]{2,1,0:T(8,128)(2,1)S(1)} collective-permute-done((bf16[1,256,1024]{2,1,0:T(8,128)(2,1)S(1)}, bf16[1,256,1024]{2,1,0:T(8,128)(2,1)S(1)}, u32[]{:S(2)}, u32[]{:S(2)}) %collective-permute-start.5) | collective-permute-done | bytes 524320 | tf_op jit(solution)/shard_map/ppermute | solution.py:20
  186.4 6.8 copy.40
  193.2 39.2 %while.32 = (s32[]{:T(128)}, bf16[1,256,1024]{1,2,0:T(8,128)(2,1)S(1)}, bf16[1,2304,1024]{1,2,0:T(8,128)(2,1)}, bf16[1,256,1024]{1,2,0:T(8,128)(2,1)}, bf16[1,23...) while((s32[]{:T(128)}, ...), condition=%wide.region_4.5_spmd.clone, body=%wide.region_2.4_spmd.clone.sunk | while | flops 622918656 | bytes 28529072 | solution.py:76
  241.3 4.5 all-to-all-start
  255.1 5.4 all-to-all-start.1
  261.9 69.6 %psum.7 = f32[]{:T(128)} all-reduce(f32[]{:T(128)} %multiply_reduce_fusion.2), channel_id=1, replica_groups=mesh['member'=8,'band'=16] {'member','band'}, use_global_device_ids=true, to_apply=%region_19.20 | all-reduce | flops 1 | bytes 8 | tf_op jit(solution)/shard_map/psum | solution.py:237
  344.6 256.9 %while.33 = (s32[]{:T(128)}, bf16[1,256,1024]{1,2,0:T(8,128)(2,1)}, bf16[1,2304,1024]{1,2,0:T(8,128)(2,1)}, bf16[1,2304,1024]{1,2,0:T(8,128)(2,1)}, bf16[1,2304,...) while((s32[]{:T(128)}, bf16[1,256,1024]{1,2,0:T(8,128)(2,1)}, ...), condition=%wide.region_12.13_spmd.clone, body=%wide.region_9.12_spmd.clone.sunk | while | flops 1581979136 | bytes 88961552 | solution.py:136
  351.1 5.0 fusion.214
  356.2 5.5 fusion.216
  361.7 19.0 %fusion.217 = bf16[4,64,256]{2,1,0:T(8,128)(2,1)} fusion(bf16[2304,4,64]{0,2,1:T(8,128)(2,1)S(1)} %bitcast.245, f32[4,256,2304]{2,1,0:T(8,128)} %fusion.214, f32[4,256,2304]{2,1,0:T(8,128)} %get-tuple-element.631, f32[4,256]{1,0:T(4,128)} %get-tuple-element.632, pred[256,2304]{1,0:T(8,128)(4,1)} %copy-done.5), kind=kOutput, calls=%fused_computation.30.clone.1 | convolution fusion | flops 328011008 | bytes 20779008 | tf_op jit(solution)/shard_map/while/body/eval_jaxpr/mgqk,mkgd->mqgd/dot_general | solution.py:102
  380.7 19.6 %fusion.219 = bf16[4,64,2304]{2,1,0:T(8,128)(2,1)S(1)} fusion(bf16[256,4,64]{0,2,1:T(8,128)(2,1)S(1)} %bitcast.251, f32[4,256,2304]{2,1,0:T(8,128)} %fusion.214, f32[4,256,2304]{2,1,0:T(8,128)} %get-tuple-element.631, f32[4,256]{1,0:T(4,128)} %get-tuple-element.632, pred[256,2304]{1,0:T(8,128)(4,1)} %copy-done.5), kind=kOutput, calls=%fused_computation.27.clone.1 | convolution fusion | flops 328535296 | bytes 20779008 | tf_op jit(solution)/shard_map/while/body/eval_jaxpr/mgqk,mqgd->mkgd/dot_general | solution.py:105
  400.3 6.4 fusion.218
  415.3 5.0 fusion.214
  420.4 5.5 fusion.216
  425.9 19.0 %fusion.217 = bf16[4,64,256]{2,1,0:T(8,128)(2,1)} fusion(bf16[2304,4,64]{0,2,1:T(8,128)(2,1)S(1)} %bitcast.245, f32[4,256,2304]{2,1,0:T(8,128)} %fusion.214, f32[4,256,2304]{2,1,0:T(8,128)} %get-tuple-element.631, f32[4,256]{1,0:T(4,128)} %get-tuple-element.632, pred[256,2304]{1,0:T(8,128)(4,1)} %copy-done.5), kind=kOutput, calls=%fused_computation.30.clone.1 | convolution fusion | flops 328011008 | bytes 20779008 | tf_op jit(solution)/shard_map/while/body/eval_jaxpr/mgqk,mkgd->mqgd/dot_general | solution.py:102
  444.9 19.6 %fusion.219 = bf16[4,64,2304]{2,1,0:T(8,128)(2,1)S(1)} fusion(bf16[256,4,64]{0,2,1:T(8,128)(2,1)S(1)} %bitcast.251, f32[4,256,2304]{2,1,0:T(8,128)} %fusion.214, f32[4,256,2304]{2,1,0:T(8,128)} %get-tuple-element.631, f32[4,256]{1,0:T(4,128)} %get-tuple-element.632, pred[256,2304]{1,0:T(8,128)(4,1)} %copy-done.5), kind=kOutput, calls=%fused_computation.27.clone.1 | convolution fusion | flops 328535296 | bytes 20779008 | tf_op jit(solution)/shard_map/while/body/eval_jaxpr/mgqk,mqgd->mkgd/dot_general | solution.py:105
  464.5 6.4 fusion.218
  479.4 5.0 fusion.214
  484.5 5.5 fusion.216
  490.0 19.0 %fusion.217 = bf16[4,64,256]{2,1,0:T(8,128)(2,1)} fusion(bf16[2304,4,64]{0,2,1:T(8,128)(2,1)S(1)} %bitcast.245, f32[4,256,2304]{2,1,0:T(8,128)} %fusion.214, f32[4,256,2304]{2,1,0:T(8,128)} %get-tuple-element.631, f32[4,256]{1,0:T(4,128)} %get-tuple-element.632, pred[256,2304]{1,0:T(8,128)(4,1)} %copy-done.5), kind=kOutput, calls=%fused_computation.30.clone.1 | convolution fusion | flops 328011008 | bytes 20779008 | tf_op jit(solution)/shard_map/while/body/eval_jaxpr/mgqk,mkgd->mqgd/dot_general | solution.py:102
  509.0 19.6 %fusion.219 = bf16[4,64,2304]{2,1,0:T(8,128)(2,1)S(1)} fusion(bf16[256,4,64]{0,2,1:T(8,128)(2,1)S(1)} %bitcast.251, f32[4,256,2304]{2,1,0:T(8,128)} %fusion.214, f32[4,256,2304]{2,1,0:T(8,128)} %get-tuple-element.631, f32[4,256]{1,0:T(4,128)} %get-tuple-element.632, pred[256,2304]{1,0:T(8,128)(4,1)} %copy-done.5), kind=kOutput, calls=%fused_computation.27.clone.1 | convolution fusion | flops 328535296 | bytes 20779008 | tf_op jit(solution)/shard_map/while/body/eval_jaxpr/mgqk,mqgd->mkgd/dot_general | solution.py:105
  528.6 6.4 fusion.218
  543.5 5.0 fusion.214
  548.6 5.5 fusion.216
  554.1 19.0 %fusion.217 = bf16[4,64,256]{2,1,0:T(8,128)(2,1)} fusion(bf16[2304,4,64]{0,2,1:T(8,128)(2,1)S(1)} %bitcast.245, f32[4,256,2304]{2,1,0:T(8,128)} %fusion.214, f32[4,256,2304]{2,1,0:T(8,128)} %get-tuple-element.631, f32[4,256]{1,0:T(4,128)} %get-tuple-element.632, pred[256,2304]{1,0:T(8,128)(4,1)} %copy-done.5), kind=kOutput, calls=%fused_computation.30.clone.1 | convolution fusion | flops 328011008 | bytes 20779008 | tf_op jit(solution)/shard_map/while/body/eval_jaxpr/mgqk,mkgd->mqgd/dot_general | solution.py:102
  573.1 19.6 %fusion.219 = bf16[4,64,2304]{2,1,0:T(8,128)(2,1)S(1)} fusion(bf16[256,4,64]{0,2,1:T(8,128)(2,1)S(1)} %bitcast.251, f32[4,256,2304]{2,1,0:T(8,128)} %fusion.214, f32[4,256,2304]{2,1,0:T(8,128)} %get-tuple-element.631, f32[4,256]{1,0:T(4,128)} %get-tuple-element.632, pred[256,2304]{1,0:T(8,128)(4,1)} %copy-done.5), kind=kOutput, calls=%fused_computation.27.clone.1 | convolution fusion | flops 328535296 | bytes 20779008 | tf_op jit(solution)/shard_map/while/body/eval_jaxpr/mgqk,mqgd->mkgd/dot_general | solution.py:105
  592.7 6.4 fusion.218
  603.4 4.5 fusion.133
  622.4 4.8 collective-permute-start.27
  627.2 4.5 collective-permute-start.25
  631.7 13.0 %all-gather = bf16[512,128]{1,0:T(8,128)(2,1)S(1)} all-gather(bf16[64,128]{1,0:T(8,128)(2,1)} %reduce-scatter.2.cloned.1.call-done), channel_id=2, replica_groups=mesh['member'=8,'band'=16] {'member'}, dimensions={0}, use_global_device_ids=true | all-gather | bytes 147456 | tf_op jit(solution)/shard_map/all_gather | solution.py:246
  650.0 6.3 collective-permute-start.26
  662.0 17.1 %collective-permute-done.26 = bf16[1,256,1024]{1,2,0:T(8,128)(2,1)S(1)} collective-permute-done((bf16[1,256,1024]{1,2,0:T(8,128)(2,1)}, bf16[1,256,1024]{1,2,0:T(8,128)(2,1)S(1)}, u32[]{:S(2)}, u32[]{:S(2)}) %collective-permute-start.26) | collective-permute-done | bytes 524320 | tf_op jit(solution)/shard_map/ppermute | solution.py:20
  679.1 10.4 %collective-permute-start.24 = (bf16[1,256,1024]{1,2,0:T(8,128)(2,1)S(1)}, bf16[1,256,1024]{1,2,0:T(8,128)(2,1)S(1)}, u32[]{:S(2)}, u32[]{:S(2)}) collective-permute-start(bf16[1,256,1024]{1,2,0:T(8,128)(2,1)S(1)} %copy-done.23), channel_id=1, source_target_pairs={{0,1},{1,2},{2,3},{3,4},{4,5},{5,6},{6,7},{7,8},{8,9},{9,10},{10,1... | collective-permute-start | bytes 1572872 | tf_op jit(solution)/shard_map/ppermute | solution.py:20
  693.6 18.1 %collective-permute-done.24 = bf16[1,256,1024]{1,2,0:T(8,128)(2,1)S(1)} collective-permute-done((bf16[1,256,1024]{1,2,0:T(8,128)(2,1)S(1)}, bf16[1,256,1024]{1,2,0:T(8,128)(2,1)S(1)}, u32[]{:S(2)}, u32[]{:S(2)}) %collective-permute-start.24) | collective-permute-done | bytes 524320 | tf_op jit(solution)/shard_map/ppermute | solution.py:20
  717.7 9.2 %collective-permute-done.22 = bf16[1,256,1024]{1,2,0:T(8,128)(2,1)S(1)} collective-permute-done((bf16[1,256,1024]{1,2,0:T(8,128)(2,1)S(1)}, bf16[1,256,1024]{1,2,0:T(8,128)(2,1)S(1)}, u32[]{:S(2)}, u32[]{:S(2)}) %collective-permute-start.22) | collective-permute-done | bytes 524320 | tf_op jit(solution)/shard_map/ppermute | solution.py:20
  731.8 14.1 %collective-permute-done.20 = bf16[1,256,1024]{1,2,0:T(8,128)(2,1)S(1)} collective-permute-done((bf16[1,256,1024]{1,2,0:T(8,128)(2,1)S(1)}, bf16[1,256,1024]{1,2,0:T(8,128)(2,1)S(1)}, u32[]{:S(2)}, u32[]{:S(2)}) %collective-permute-start.20) | collective-permute-done | bytes 524320 | tf_op jit(solution)/shard_map/ppermute | solution.py:20
  748.1 8.1 %collective-permute-start.30 = (bf16[1,256,1024]{1,2,0:T(8,128)(2,1)S(1)}, bf16[1,256,1024]{1,2,0:T(8,128)(2,1)S(1)}, u32[]{:S(2)}, u32[]{:S(2)}) collective-permute-start(bf16[1,256,1024]{1,2,0:T(8,128)(2,1)S(1)} %copy-done.17), channel_id=1, source_target_pairs={{0,4},{1,5},{2,6},{3,7},{4,8},{5,9},{6,10},{7,11},{8,12},{9,13},{1... | collective-permute-start | bytes 1572872 | tf_op jit(solution)/shard_map/ppermute | solution.py:20
  757.0 10.2 %collective-permute-done.18 = bf16[1,256,1024]{1,2,0:T(8,128)(2,1)S(1)} collective-permute-done((bf16[1,256,1024]{1,2,0:T(8,128)(2,1)S(1)}, bf16[1,256,1024]{1,2,0:T(8,128)(2,1)S(1)}, u32[]{:S(2)}, u32[]{:S(2)}) %collective-permute-start.18) | collective-permute-done | bytes 524320 | tf_op jit(solution)/shard_map/ppermute | solution.py:20
  (302 shorter events, 241.7 us)
Async XLA Ops:
  7.2 34.2 %copy-start.7 = (bf16[1,256,1024]{2,1,0:T(8,128)(2,1)S(1)}, bf16[1,256,1024]{2,1,0:T(8,128)(2,1)}, u32[]{:S(2)}) copy-start(bf16[1,256,1024]{2,1,0:T(8,128)(2,1)} %param.15) | copy-start | bytes 1572868
  7.2 34.2 %copy-start.31 = (f32[1024]{0:T(1024)S(1)}, f32[1024]{0:T(1024)}, u32[]{:S(2)}) copy-start(f32[1024]{0:T(1024)} %param.19) | copy-start | bytes 12292
  9.2 35.3 %copy-start.34 = (f32[256]{0:T(256)}, f32[256]{0:T(256)S(1)}, u32[]{:S(2)}) copy-start(f32[256]{0:T(256)S(1)} %get-tuple-element.465) | copy-start | bytes 3076
  9.2 40.5 %copy-start.36 = (f32[256]{0:T(256)S(1)}, f32[256]{0:T(256)}, u32[]{:S(2)}) copy-start(f32[256]{0:T(256)} %param.17) | copy-start | bytes 3076
  11.8 115.1 %collective-permute-start.15 = (bf16[1,256,1024]{2,1,0:T(8,128)(2,1)}, bf16[1,256,1024]{2,1,0:T(8,128)(2,1)S(1)}, u32[]{:S(2)}, u32[]{:S(2)}) collective-permute-start(bf16[1,256,1024]{2,1,0:T(8,128)(2,1)} %fusion.73), channel_id=1, source_target_pairs={{4,0},{5,1},{6,2},{7,3},{8,4},{9,5},{10,6},{11,7},{12,8},{13,9},{1... | collective-permute-start | bytes 1572872 | tf_op jit(solution)/shard_map/ppermute | solution.py:20
  13.1 69.9 %collective-permute-start.11 = (bf16[1,256,1024]{2,1,0:T(8,128)(2,1)}, bf16[1,256,1024]{2,1,0:T(8,128)(2,1)}, u32[]{:S(2)}, u32[]{:S(2)}) collective-permute-start(bf16[1,256,1024]{2,1,0:T(8,128)(2,1)} %fusion.73), channel_id=1, source_target_pairs={{0,1},{1,2},{2,3},{3,4},{4,5},{5,6},{6,7},{7,8},{8,9},{9,10},{10,1... | collective-permute-start | bytes 1572872 | tf_op jit(solution)/shard_map/ppermute | solution.py:20
  16.3 62.9 %collective-permute-start.10 = (bf16[1,256,1024]{2,1,0:T(8,128)(2,1)}, bf16[1,256,1024]{2,1,0:T(8,128)(2,1)}, u32[]{:S(2)}, u32[]{:S(2)}) collective-permute-start(bf16[1,256,1024]{2,1,0:T(8,128)(2,1)} %fusion.73), channel_id=1, source_target_pairs={{0,2},{1,3},{2,4},{3,5},{4,6},{5,7},{6,8},{7,9},{8,10},{9,11},{10,... | collective-permute-start | bytes 1572872 | tf_op jit(solution)/shard_map/ppermute | solution.py:20
  20.9 54.5 %collective-permute-start.9 = (bf16[1,256,1024]{2,1,0:T(8,128)(2,1)}, bf16[1,256,1024]{2,1,0:T(8,128)(2,1)}, u32[]{:S(2)}, u32[]{:S(2)}) collective-permute-start(bf16[1,256,1024]{2,1,0:T(8,128)(2,1)} %fusion.73), channel_id=1, source_target_pairs={{0,3},{1,4},{2,5},{3,6},{4,7},{5,8},{6,9},{7,10},{8,11},{9,12},{10... | collective-permute-start | bytes 1572872 | tf_op jit(solution)/shard_map/ppermute | solution.py:20
  25.6 43.5 %collective-permute-start.8 = (bf16[1,256,1024]{2,1,0:T(8,128)(2,1)}, bf16[1,256,1024]{2,1,0:T(8,128)(2,1)}, u32[]{:S(2)}, u32[]{:S(2)}) collective-permute-start(bf16[1,256,1024]{2,1,0:T(8,128)(2,1)} %fusion.73), channel_id=1, source_target_pairs={{0,4},{1,5},{2,6},{3,7},{4,8},{5,9},{6,10},{7,11},{8,12},{9,13},{1... | collective-permute-start | bytes 1572872 | tf_op jit(solution)/shard_map/ppermute | solution.py:20
  44.5 43.5 %copy-start.24 = (bf16[1,256,1024]{2,1,0:T(8,128)(2,1)S(1)}, bf16[1,256,1024]{2,1,0:T(8,128)(2,1)}, u32[]{:S(2)}) copy-start(bf16[1,256,1024]{2,1,0:T(8,128)(2,1)} %fusion.71) | copy-start | bytes 1572868
  69.1 18.9 %collective-permute-start = (bf16[1,256,1024]{2,1,0:T(8,128)(2,1)}, bf16[1,256,1024]{2,1,0:T(8,128)(2,1)S(1)}, u32[]{:S(2)}, u32[]{:S(2)}) collective-permute-start(bf16[1,256,1024]{2,1,0:T(8,128)(2,1)} %fusion.71), channel_id=1, source_target_pairs={{0,4},{1,5},{2,6},{3,7},{4,8},{5,9},{6,10},{7,11},{8,12},{9,13},{1... | collective-permute-start | bytes 1572872 | tf_op jit(solution)/shard_map/ppermute | solution.py:20
  75.4 24.8 %collective-permute-start.12 = (bf16[1,256,1024]{2,1,0:T(8,128)(2,1)}, bf16[1,256,1024]{2,1,0:T(8,128)(2,1)S(1)}, u32[]{:S(2)}, u32[]{:S(2)}) collective-permute-start(bf16[1,256,1024]{2,1,0:T(8,128)(2,1)} %fusion.73), channel_id=1, source_target_pairs={{1,0},{2,1},{3,2},{4,3},{5,4},{6,5},{7,6},{8,7},{9,8},{10,9},{11,1... | collective-permute-start | bytes 1572872 | tf_op jit(solution)/shard_map/ppermute | solution.py:20
  79.2 42.1 %collective-permute-start.13 = (bf16[1,256,1024]{2,1,0:T(8,128)(2,1)}, bf16[1,256,1024]{2,1,0:T(8,128)(2,1)S(1)}, u32[]{:S(2)}, u32[]{:S(2)}) collective-permute-start(bf16[1,256,1024]{2,1,0:T(8,128)(2,1)} %fusion.73), channel_id=1, source_target_pairs={{2,0},{3,1},{4,2},{5,3},{6,4},{7,5},{8,6},{9,7},{10,8},{11,9},{12,... | collective-permute-start | bytes 1572872 | tf_op jit(solution)/shard_map/ppermute | solution.py:20
  83.0 41.7 %collective-permute-start.14 = (bf16[1,256,1024]{2,1,0:T(8,128)(2,1)}, bf16[1,256,1024]{2,1,0:T(8,128)(2,1)S(1)}, u32[]{:S(2)}, u32[]{:S(2)}) collective-permute-start(bf16[1,256,1024]{2,1,0:T(8,128)(2,1)} %fusion.73), channel_id=1, source_target_pairs={{3,0},{4,1},{5,2},{6,3},{7,4},{8,5},{9,6},{10,7},{11,8},{12,9},{13... | collective-permute-start | bytes 1572872 | tf_op jit(solution)/shard_map/ppermute | solution.py:20
  88.0 46.4 %collective-permute-start.1 = (bf16[1,256,1024]{2,1,0:T(8,128)(2,1)S(1)}, bf16[1,256,1024]{2,1,0:T(8,128)(2,1)S(1)}, u32[]{:S(2)}, u32[]{:S(2)}) collective-permute-start(bf16[1,256,1024]{2,1,0:T(8,128)(2,1)S(1)} %copy-done.24), channel_id=1, source_target_pairs={{0,3},{1,4},{2,5},{3,6},{4,7},{5,8},{6,9},{7,10},{8,11},{9,12},{10... | collective-permute-start | bytes 1572872 | tf_op jit(solution)/shard_map/ppermute | solution.py:20
  100.3 40.0 %collective-permute-start.2 = (bf16[1,256,1024]{2,1,0:T(8,128)(2,1)S(1)}, bf16[1,256,1024]{2,1,0:T(8,128)(2,1)S(1)}, u32[]{:S(2)}, u32[]{:S(2)}) collective-permute-start(bf16[1,256,1024]{2,1,0:T(8,128)(2,1)S(1)} %copy-done.24), channel_id=1, source_target_pairs={{0,2},{1,3},{2,4},{3,5},{4,6},{5,7},{6,8},{7,9},{8,10},{9,11},{10,... | collective-permute-start | bytes 1572872 | tf_op jit(solution)/shard_map/ppermute | solution.py:20
  121.3 25.3 %collective-permute-start.3 = (bf16[1,256,1024]{2,1,0:T(8,128)(2,1)S(1)}, bf16[1,256,1024]{2,1,0:T(8,128)(2,1)S(1)}, u32[]{:S(2)}, u32[]{:S(2)}) collective-permute-start(bf16[1,256,1024]{2,1,0:T(8,128)(2,1)S(1)} %copy-done.24), channel_id=1, source_target_pairs={{0,1},{1,2},{2,3},{3,4},{4,5},{5,6},{6,7},{7,8},{8,9},{9,10},{10,1... | collective-permute-start | bytes 1572872 | tf_op jit(solution)/shard_map/ppermute | solution.py:20
  124.7 59.8 %collective-permute-start.7 = (bf16[1,256,1024]{2,1,0:T(8,128)(2,1)S(1)}, bf16[1,256,1024]{2,1,0:T(8,128)(2,1)}, u32[]{:S(2)}, u32[]{:S(2)}) collective-permute-start(bf16[1,256,1024]{2,1,0:T(8,128)(2,1)S(1)} %copy-done.24), channel_id=1, source_target_pairs={{4,0},{5,1},{6,2},{7,3},{8,4},{9,5},{10,6},{11,7},{12,8},{13,9},{1... | collective-permute-start | bytes 1572872 | tf_op jit(solution)/shard_map/ppermute | solution.py:20
  126.9 28.1 %collective-permute-start.4 = (bf16[1,256,1024]{2,1,0:T(8,128)(2,1)S(1)}, bf16[1,256,1024]{2,1,0:T(8,128)(2,1)}, u32[]{:S(2)}, u32[]{:S(2)}) collective-permute-start(bf16[1,256,1024]{2,1,0:T(8,128)(2,1)S(1)} %copy-done.24), channel_id=1, source_target_pairs={{1,0},{2,1},{3,2},{4,3},{5,4},{6,5},{7,6},{8,7},{9,8},{10,9},{11,1... | collective-permute-start | bytes 1572872 | tf_op jit(solution)/shard_map/ppermute | solution.py:20
  134.4 47.4 %collective-permute-start.5 = (bf16[1,256,1024]{2,1,0:T(8,128)(2,1)S(1)}, bf16[1,256,1024]{2,1,0:T(8,128)(2,1)S(1)}, u32[]{:S(2)}, u32[]{:S(2)}) collective-permute-start(bf16[1,256,1024]{2,1,0:T(8,128)(2,1)S(1)} %copy-done.24), channel_id=1, source_target_pairs={{2,0},{3,1},{4,2},{5,3},{6,4},{7,5},{8,6},{9,7},{10,8},{11,9},{12,... | collective-permute-start | bytes 1572872 | tf_op jit(solution)/shard_map/ppermute | solution.py:20
  140.2 42.5 %collective-permute-start.6 = (bf16[1,256,1024]{2,1,0:T(8,128)(2,1)S(1)}, bf16[1,256,1024]{2,1,0:T(8,128)(2,1)}, u32[]{:S(2)}, u32[]{:S(2)}) collective-permute-start(bf16[1,256,1024]{2,1,0:T(8,128)(2,1)S(1)} %copy-done.24), channel_id=1, source_target_pairs={{3,0},{4,1},{5,2},{6,3},{7,4},{8,5},{9,6},{10,7},{11,8},{12,9},{13... | collective-permute-start | bytes 1572872 | tf_op jit(solution)/shard_map/ppermute | solution.py:20
  193.2 43.9 %copy-start.14 = (bf16[1024,128]{1,0:T(8,128)(2,1)S(1)}, bf16[1024,128]{1,0:T(8,128)(2,1)}, u32[]{:S(2)}) copy-start(bf16[1024,128]{1,0:T(8,128)(2,1)} %param.25) | copy-start | bytes 786436
  193.2 43.9 %copy-start.25 = (f32[1024]{0:T(1024)S(1)}, f32[1024]{0:T(1024)}, u32[]{:S(2)}) copy-start(f32[1024]{0:T(1024)} %param.24) | copy-start | bytes 12292
  235.9 102.9 %copy-start.3 = (f32[1,256,1024]{2,1,0:T(8,128)}, f32[1,256,1024]{2,1,0:T(8,128)S(1)}, u32[]{:S(2)}) copy-start(f32[1,256,1024]{2,1,0:T(8,128)S(1)} %get-tuple-element.489) | copy-start | bytes 3145732
  241.3 8.1 %all-to-all-start = ((bf16[8,2,2048]{2,1,0:T(2,128)(2,1)}), bf16[8,2,2048]{2,1,0:T(2,128)(2,1)S(1)}, u32[]{:S(2)}, u32[]{:S(2)}) async-start(bf16[8,2,2048]{2,1,0:T(2,128)(2,1)} %reshape.534), calls=%async_computation | async-start | bytes 131072 | tf_op jit(solution)/shard_map/all_to_all | solution.py:224
  255.1 76.4 %all-to-all-start.1 = ((bf16[8,32,128]{2,1,0:T(8,128)(2,1)}), bf16[8,32,128]{2,1,0:T(8,128)(2,1)S(1)}, u32[]{:S(2)}, u32[]{:S(2)}) async-start(bf16[8,32,128]{2,1,0:T(8,128)(2,1)} %get-tuple-element.463), calls=%async_computation.1 | async-start | bytes 131072 | tf_op jit(solution)/shard_map/all_to_all | solution.py:234
  260.4 371.3 %reduce-scatter.2.cloned.1.call-start = ((), (), s32[]{:S(2)}) async-start(), calls=%async_computation.3 | async-start | bytes 278528 | tf_op jit(solution)/shard_map/reduce_scatter | solution.py:238
  611.0 34.4 %collective-permute-start.29 = (bf16[1,256,1024]{1,2,0:T(8,128)(2,1)}, bf16[1,256,1024]{1,2,0:T(8,128)(2,1)}, u32[]{:S(2)}, u32[]{:S(2)}) collective-permute-start(bf16[1,256,1024]{1,2,0:T(8,128)(2,1)} %get-tuple-element.455), channel_id=1, source_target_pairs={{0,3},{1,4},{2,5},{3,6},{4,7},{5,8},{6,9},{7,10},{8,11},{9,12},{10... | collective-permute-start | bytes 1572872 | tf_op jit(solution)/shard_map/ppermute | solution.py:20
  617.4 32.6 %collective-permute-start.28 = (bf16[1,256,1024]{1,2,0:T(8,128)(2,1)}, bf16[1,256,1024]{1,2,0:T(8,128)(2,1)}, u32[]{:S(2)}, u32[]{:S(2)}) collective-permute-start(bf16[1,256,1024]{1,2,0:T(8,128)(2,1)} %get-tuple-element.447), channel_id=1, source_target_pairs={{0,3},{1,4},{2,5},{3,6},{4,7},{5,8},{6,9},{7,10},{8,11},{9,12},{10... | collective-permute-start | bytes 1572872 | tf_op jit(solution)/shard_map/ppermute | solution.py:20
  621.1 146.9 %collective-permute-start.17 = (bf16[1,256,1024]{1,2,0:T(8,128)(2,1)}, bf16[1,256,1024]{1,2,0:T(8,128)(2,1)}, u32[]{:S(2)}, u32[]{:S(2)}) collective-permute-start(bf16[1,256,1024]{1,2,0:T(8,128)(2,1)} %get-tuple-element.454), channel_id=1, source_target_pairs={{4,0},{5,1},{6,2},{7,3},{8,4},{9,5},{10,6},{11,7},{12,8},{13,9},{1... | collective-permute-start | bytes 1572872 | tf_op jit(solution)/shard_map/ppermute | solution.py:20
  622.4 35.7 %collective-permute-start.27 = (bf16[1,256,1024]{1,2,0:T(8,128)(2,1)}, bf16[1,256,1024]{1,2,0:T(8,128)(2,1)}, u32[]{:S(2)}, u32[]{:S(2)}) collective-permute-start(bf16[1,256,1024]{1,2,0:T(8,128)(2,1)} %get-tuple-element.456), channel_id=1, source_target_pairs={{0,2},{1,3},{2,4},{3,5},{4,6},{5,7},{6,8},{7,9},{8,10},{9,11},{10,... | collective-permute-start | bytes 1572872 | tf_op jit(solution)/shard_map/ppermute | solution.py:20
  627.2 63.2 %collective-permute-start.25 = (bf16[1,256,1024]{1,2,0:T(8,128)(2,1)}, bf16[1,256,1024]{1,2,0:T(8,128)(2,1)}, u32[]{:S(2)}, u32[]{:S(2)}) collective-permute-start(bf16[1,256,1024]{1,2,0:T(8,128)(2,1)} %get-tuple-element.457), channel_id=1, source_target_pairs={{0,1},{1,2},{2,3},{3,4},{4,5},{5,6},{6,7},{7,8},{8,9},{9,10},{10,1... | collective-permute-start | bytes 1572872 | tf_op jit(solution)/shard_map/ppermute | solution.py:20
  645.4 69.1 %collective-permute-start.23 = (bf16[1,256,1024]{1,2,0:T(8,128)(2,1)}, bf16[1,256,1024]{1,2,0:T(8,128)(2,1)S(1)}, u32[]{:S(2)}, u32[]{:S(2)}) collective-permute-start(bf16[1,256,1024]{1,2,0:T(8,128)(2,1)} %get-tuple-element.458), channel_id=1, source_target_pairs={{1,0},{2,1},{3,2},{4,3},{5,4},{6,5},{7,6},{8,7},{9,8},{10,9},{11,1... | collective-permute-start | bytes 1572872 | tf_op jit(solution)/shard_map/ppermute | solution.py:20
  649.9 29.2 %copy-start.23 = (bf16[1,256,1024]{1,2,0:T(8,128)(2,1)S(1)}, bf16[1,256,1024]{1,2,0:T(8,128)(2,1)}, u32[]{:S(2)}) copy-start(bf16[1,256,1024]{1,2,0:T(8,128)(2,1)} %get-tuple-element.449) | copy-start | bytes 1572868
  650.0 29.1 %collective-permute-start.26 = (bf16[1,256,1024]{1,2,0:T(8,128)(2,1)}, bf16[1,256,1024]{1,2,0:T(8,128)(2,1)S(1)}, u32[]{:S(2)}, u32[]{:S(2)}) collective-permute-start(bf16[1,256,1024]{1,2,0:T(8,128)(2,1)} %get-tuple-element.448), channel_id=1, source_target_pairs={{0,2},{1,3},{2,4},{3,5},{4,6},{5,7},{6,8},{7,9},{8,10},{9,11},{10,... | collective-permute-start | bytes 1572872 | tf_op jit(solution)/shard_map/ppermute | solution.py:20
  658.1 32.3 %copy-start.18 = (bf16[1,256,1024]{1,2,0:T(8,128)(2,1)S(1)}, bf16[1,256,1024]{1,2,0:T(8,128)(2,1)}, u32[]{:S(2)}) copy-start(bf16[1,256,1024]{1,2,0:T(8,128)(2,1)} %get-tuple-element.460) | copy-start | bytes 1572868
  658.1 71.5 %collective-permute-start.21 = (bf16[1,256,1024]{1,2,0:T(8,128)(2,1)S(1)}, bf16[1,256,1024]{1,2,0:T(8,128)(2,1)S(1)}, u32[]{:S(2)}, u32[]{:S(2)}) collective-permute-start(bf16[1,256,1024]{1,2,0:T(8,128)(2,1)S(1)} %copy-done.20), channel_id=1, source_target_pairs={{2,0},{3,1},{4,2},{5,3},{6,4},{7,5},{8,6},{9,7},{10,8},{11,9},{12,... | collective-permute-start | bytes 1572872 | tf_op jit(solution)/shard_map/ppermute | solution.py:20
  662.0 49.7 %copy-start.22 = (bf16[1,256,1024]{1,2,0:T(8,128)(2,1)S(1)}, bf16[1,256,1024]{1,2,0:T(8,128)(2,1)}, u32[]{:S(2)}) copy-start(bf16[1,256,1024]{1,2,0:T(8,128)(2,1)} %get-tuple-element.450) | copy-start | bytes 1572868
  679.1 32.6 %collective-permute-start.24 = (bf16[1,256,1024]{1,2,0:T(8,128)(2,1)S(1)}, bf16[1,256,1024]{1,2,0:T(8,128)(2,1)S(1)}, u32[]{:S(2)}, u32[]{:S(2)}) collective-permute-start(bf16[1,256,1024]{1,2,0:T(8,128)(2,1)S(1)} %copy-done.23), channel_id=1, source_target_pairs={{0,1},{1,2},{2,3},{3,4},{4,5},{5,6},{6,7},{7,8},{8,9},{9,10},{10,1... | collective-permute-start | bytes 1572872 | tf_op jit(solution)/shard_map/ppermute | solution.py:20
  690.4 57.7 %collective-permute-start.19 = (bf16[1,256,1024]{1,2,0:T(8,128)(2,1)S(1)}, bf16[1,256,1024]{1,2,0:T(8,128)(2,1)S(1)}, u32[]{:S(2)}, u32[]{:S(2)}) collective-permute-start(bf16[1,256,1024]{1,2,0:T(8,128)(2,1)S(1)} %copy-done.18), channel_id=1, source_target_pairs={{3,0},{4,1},{5,2},{6,3},{7,4},{8,5},{9,6},{10,7},{11,8},{12,9},{13... | collective-permute-start | bytes 1572872 | tf_op jit(solution)/shard_map/ppermute | solution.py:20
  693.6 33.3 %copy-start.21 = (bf16[1,256,1024]{1,2,0:T(8,128)(2,1)S(1)}, bf16[1,256,1024]{1,2,0:T(8,128)(2,1)}, u32[]{:S(2)}) copy-start(bf16[1,256,1024]{1,2,0:T(8,128)(2,1)} %get-tuple-element.451) | copy-start | bytes 1572868
  711.7 15.2 %collective-permute-start.22 = (bf16[1,256,1024]{1,2,0:T(8,128)(2,1)S(1)}, bf16[1,256,1024]{1,2,0:T(8,128)(2,1)S(1)}, u32[]{:S(2)}, u32[]{:S(2)}) collective-permute-start(bf16[1,256,1024]{1,2,0:T(8,128)(2,1)S(1)} %copy-done.22), channel_id=1, source_target_pairs={{1,0},{2,1},{3,2},{4,3},{5,4},{6,5},{7,6},{8,7},{9,8},{10,9},{11,1... | collective-permute-start | bytes 1572872 | tf_op jit(solution)/shard_map/ppermute | solution.py:20
  714.5 55.3 %collective-permute-start.31 = (bf16[1,256,1024]{1,2,0:T(8,128)(2,1)S(1)}, bf16[1,256,1024]{1,2,0:T(8,128)(2,1)S(1)}, u32[]{:S(2)}, u32[]{:S(2)}) collective-permute-start(bf16[1,256,1024]{1,2,0:T(8,128)(2,1)S(1)} %copy-done.15), channel_id=1, source_target_pairs={{0,4},{1,5},{2,6},{3,7},{4,8},{5,9},{6,10},{7,11},{8,12},{9,13},{1... | collective-permute-start | bytes 1572872 | tf_op jit(solution)/shard_map/ppermute | solution.py:20
  717.7 28.3 %copy-start.19 = (bf16[1,256,1024]{1,2,0:T(8,128)(2,1)S(1)}, bf16[1,256,1024]{1,2,0:T(8,128)(2,1)}, u32[]{:S(2)}) copy-start(bf16[1,256,1024]{1,2,0:T(8,128)(2,1)} %get-tuple-element.452) | copy-start | bytes 1572868
  726.9 19.1 %collective-permute-start.20 = (bf16[1,256,1024]{1,2,0:T(8,128)(2,1)S(1)}, bf16[1,256,1024]{1,2,0:T(8,128)(2,1)S(1)}, u32[]{:S(2)}, u32[]{:S(2)}) collective-permute-start(bf16[1,256,1024]{1,2,0:T(8,128)(2,1)S(1)} %copy-done.21), channel_id=1, source_target_pairs={{2,0},{3,1},{4,2},{5,3},{6,4},{7,5},{8,6},{9,7},{10,8},{11,9},{12,... | collective-permute-start | bytes 1572872 | tf_op jit(solution)/shard_map/ppermute | solution.py:20
  729.6 41.8 %collective-permute-start.16 = (bf16[1,256,1024]{1,2,0:T(8,128)(2,1)S(1)}, bf16[1,256,1024]{1,2,0:T(8,128)(2,1)S(1)}, u32[]{:S(2)}, u32[]{:S(2)}) collective-permute-start(bf16[1,256,1024]{1,2,0:T(8,128)(2,1)S(1)} %copy-done.16), channel_id=1, source_target_pairs={{4,0},{5,1},{6,2},{7,3},{8,4},{9,5},{10,6},{11,7},{12,8},{13,9},{1... | collective-permute-start | bytes 1572872 | tf_op jit(solution)/shard_map/ppermute | solution.py:20
  746.0 21.2 %collective-permute-start.18 = (bf16[1,256,1024]{1,2,0:T(8,128)(2,1)S(1)}, bf16[1,256,1024]{1,2,0:T(8,128)(2,1)S(1)}, u32[]{:S(2)}, u32[]{:S(2)}) collective-permute-start(bf16[1,256,1024]{1,2,0:T(8,128)(2,1)S(1)} %copy-done.19), channel_id=1, source_target_pairs={{3,0},{4,1},{5,2},{6,3},{7,4},{8,5},{9,6},{10,7},{11,8},{12,9},{13... | collective-permute-start | bytes 1572872 | tf_op jit(solution)/shard_map/ppermute | solution.py:20
  748.1 22.5 %collective-permute-start.30 = (bf16[1,256,1024]{1,2,0:T(8,128)(2,1)S(1)}, bf16[1,256,1024]{1,2,0:T(8,128)(2,1)S(1)}, u32[]{:S(2)}, u32[]{:S(2)}) collective-permute-start(bf16[1,256,1024]{1,2,0:T(8,128)(2,1)S(1)} %copy-done.17), channel_id=1, source_target_pairs={{0,4},{1,5},{2,6},{3,7},{4,8},{5,9},{6,10},{7,11},{8,12},{9,13},{1... | collective-permute-start | bytes 1572872 | tf_op jit(solution)/shard_map/ppermute | solution.py:20
  (32 other events, 217.9 us)
Sparse Core Ops, SparseCore 0:
  335.4 72.1 reduce-scatter.1
